TPU v7x, 512 devices: a whole 4x8x8 slice. The times are simulated.
512 devices in a mesh: rep: 128 (over y, z, core), tp: 4 (over x).
Axes of the slice: x: 4, y: 8, z: 8, core: 2. Of those that a mesh axis runs over, the one named last changes fastest.
Arguments:
- gradients: bfloat16 [128, 1024, 1024], P('rep', None, 'tp'), may hold values from -24 to 24
- feedback: float32 [128, 1024, 1024], P('rep', None, 'tp'), may hold values from -4 to 4
- warm_factor: float32 [1024, 32], P('tp'), may hold values from -0.1875 to 0.1875
- momentum: float32 [1024, 1024], P('rep', 'tp'), may hold values from -3 to 3
- master_owned: float32 [1024, 1024], P('rep', 'tp'), may hold values from -4 to 4
- vector_grads: float32 [128, 2560], P('rep'), may hold values from -6 to 6
- vector_params: float32 [2560], replicated, may hold values from 0.5 to 1.5
- vector_momentum: float32 [2560], replicated, may hold values from -3 to 3
Outputs:
- new_feedback: float32 [128, 1024, 1024], P('rep', None, 'tp')
- new_momentum: float32 [1024, 1024], P('rep', 'tp')
- new_master: float32 [1024, 1024], P('rep', 'tp')
- weight: bfloat16 [1024, 1024], P(None, 'tp')
- new_vector_params: float32 [2560], replicated
- new_vector_momentum: float32 [2560], replicated
All inputs are finite; a program needn't handle non-finite values.
Results may differ from a plain program's by a relative error of at most 0.0049.
Values may be sent and summed in bfloat16 or wider, within the bound.
No kernel may reach another device: no remote copies, remote signals or barrier semaphores. Data moves between devices by JAX's collectives and lax.ppermute only.
A program may use at most 64 MiB of HBM per device.

v0:
```python
import jax
import jax.numpy as jnp
from jax import lax
from jax.sharding import Mesh
from jax.sharding import PartitionSpec as P

REP = ("rep_0", "rep_1", "rep_2")


PRECISE = lax.Precision.HIGHEST
MOMENTUM_RATE = 0.9
LEARN_RATE = 0.5


def in_blocks(array, dim, peers):
    before, after = (array.shape[:dim], array.shape[dim + 1 :])
    return jnp.moveaxis(array.reshape(*before, peers, -1, *after), dim, 0)


def sent_and_summed(array, axis, dim):
    peers = lax.axis_size(axis)
    pieces = lax.all_to_all(in_blocks(array, dim, peers), axis, 0, 0, tiled=True)
    return jnp.sum(pieces.astype(jnp.float32), axis=0)


def sent_and_summed_2(array, axis, dim):
    peers = lax.axis_size(axis)
    pieces = lax.all_to_all(in_blocks(array, dim, peers), axis, 0, 0, tiled=True)
    return jnp.sum(pieces, axis=0)


def sum_by_axis(array, axes, dim):
    far, near = axes
    pieces = in_blocks(array, dim, lax.axis_size(far))
    nearer = sent_and_summed_2(pieces, near, dim + 1)
    arrived = lax.all_to_all(nearer, far, split_axis=0, concat_axis=0, tiled=True)
    return arrived.sum(axis=0)


def filled_up(lines, peers):
    spare = -lines.shape[0] % peers
    if not spare:
        return lines
    return jnp.concatenate([lines, jnp.zeros((spare, *lines.shape[1:]), lines.dtype)])


def sent_to_all(array, axis):
    copies = jnp.broadcast_to(array, (lax.axis_size(axis), *array.shape))
    return lax.all_to_all(copies, axis, split_axis=0, concat_axis=0, tiled=True)


def in_order(pieces, dim):
    pieces = jnp.moveaxis(pieces, 0, dim)
    dims = pieces.shape
    return pieces.reshape(*dims[:dim], dims[dim] * dims[dim + 1], *dims[dim + 2 :])


def gather_axes(array, axes, dim):
    far, near = axes
    pieces = sent_to_all(sent_to_all(array, far), near)
    return in_order(pieces.swapaxes(0, 1).reshape(-1, *array.shape), dim)


def sum_by_parts(array, axes):
    lines = array.reshape(-1, array.shape[-1])
    own = sum_by_axis(filled_up(lines, lax.axis_size(axes[0]) * lax.axis_size(axes[1])), axes, 0)
    whole = gather_axes(own, axes, 0)
    return whole[: len(lines)].reshape(array.shape)


def gather_directly(array, axis, dim):
    pieces = sent_to_all(array, axis)
    return in_order(pieces, dim)


def total_of(array, axes):
    own = sum_by_axis(filled_up(array, lax.axis_size(axes[0]) * lax.axis_size(axes[1])), axes, 0)
    whole = gather_axes(own, axes, 0)
    return whole[: len(array)].reshape(array.shape)


def in_one(arrays, axis):
    ravelled, at, done = (jnp.concatenate([a.reshape(-1) for a in arrays]), 0, [])
    total = total_of(ravelled, axis)
    for a in arrays:
        done.append(total[at : at + a.size].reshape(a.shape))
        at += a.size
    return tuple(done)


def left_factor(combined, factor):
    partial_terms = jnp.dot(combined, factor, precision=PRECISE)
    shares = sent_and_summed(partial_terms.astype(jnp.bfloat16), "tp", 0)
    shares = sum_by_parts(shares, (("rep_0", "rep_1"), "rep_2"))
    return gather_directly(shares.astype(jnp.bfloat16), "tp", 0).astype(shares.dtype)


def orthonormal(left):
    gram = jnp.dot(left.T, left, precision=PRECISE)
    lower = jnp.linalg.cholesky(gram)
    return jax.scipy.linalg.solve_triangular(lower, left.T, lower=True).T


def right_terms(combined, ortho):
    return lax.dot_general(combined, ortho, (((0,), (0,)), ((), ())), precision=PRECISE)


def shards(
    gradients,
    feedback,
    warm_factor,
    momentum,
    master_owned,
    vector_grads,
    vector_params,
    vector_momentum,
):
    replicas = lax.axis_size(REP)
    combined = gradients[0].astype(jnp.float32) + feedback[0]
    left_one = left_factor(combined, warm_factor)
    ortho_one = orthonormal(left_one)
    right_one = sum_by_parts(right_terms(combined, ortho_one), (("rep_0", "rep_1"), "rep_2"))
    left_two = left_factor(combined, right_one)
    ortho_two = orthonormal(left_two)
    right_two, vector_sum = in_one(
        (right_terms(combined, ortho_two), vector_grads[0]), (("rep_0", "rep_1"), "rep_2")
    )
    approx = jnp.dot(ortho_two, right_two.T, precision=PRECISE) / replicas
    new_feedback = (combined - approx)[None]
    owned_rows = momentum.shape[0]
    row_start = lax.axis_index(REP) * owned_rows
    owned_approx = lax.dynamic_slice_in_dim(approx, row_start, owned_rows, 0)
    new_momentum = MOMENTUM_RATE * momentum + owned_approx
    new_master = master_owned - LEARN_RATE * new_momentum
    weight = gather_axes(new_master.astype(jnp.bfloat16), (("rep_0", "rep_1"), "rep_2"), 0)
    new_vector_momentum = MOMENTUM_RATE * vector_momentum + vector_sum / replicas
    new_vector_params = vector_params - LEARN_RATE * new_vector_momentum
    return (new_feedback, new_momentum, new_master, weight, new_vector_params, new_vector_momentum)


def solution(mesh):
    finer = Mesh(mesh.devices.reshape(8, 8, 2, mesh.shape["tp"]), ("rep_0", "rep_1", "rep_2", "tp"))
    in_specs = (
        P(REP, None, "tp"),
        P(REP, None, "tp"),
        P("tp", None),
        P(REP, "tp"),
        P(REP, "tp"),
        P(REP, None),
        P(),
        P(),
    )
    out_specs = (P(REP, None, "tp"), P(REP, "tp"), P(REP, "tp"), P(None, "tp"), P(), P())
    return jax.shard_map(
        shards, mesh=finer, in_specs=in_specs, out_specs=out_specs, check_vma=False
    )
```

profile of v0, /device:TPU:1, one launch (start us, length us, event | category | flops | bytes accessed | tf_op | source)
XLA Modules:
  0.0 268.2 jit_solution(3155304577860394877)
XLA Ops:
  1.4 2.5 convolution_convert_fusion.1
  3.9 9.2 %all_to_all.118 = bf16[4,256,32]{1,2,0:T(8,128)(2,1)S(1)} all-to-all(bf16[4,256,32]{1,2,0:T(8,128)(2,1)S(1)} %bitcast.135), channel_id=1, replica_groups=mesh['rep_0'=8,'rep_1'=8,'rep_2'=2,'tp'=4] {'tp'}, dimensions={0} | all-to-all | bytes 131072 | tf_op jit(solution)/shard_map/all_to_all | solution.py:22
  13.5 9.1 %all_to_all.119 = f32[2,1,4096]{2,1,0:T(1,128)S(1)} all-to-all(f32[2,1,4096]{2,1,0:T(1,128)S(1)} %reshape.59), channel_id=1, replica_groups=mesh['rep_0'=8,'rep_1'=8,'rep_2'=2,'tp'=4] {'rep_2'}, dimensions={0} | all-to-all | bytes 65536 | tf_op jit(solution)/shard_map/all_to_all | solution.py:28
  24.1 23.8 %all_to_all.120 = f32[64,2,32]{2,1,0:T(2,128)S(1)} all-to-all(f32[64,2,32]{2,1,0:T(2,128)S(1)} %copy.103), channel_id=1, replica_groups=mesh['rep_0'=8,'rep_1'=8,'rep_2'=2,'tp'=4] {'rep_0','rep_1'}, dimensions={0} | all-to-all | bytes 32768 | tf_op jit(solution)/shard_map/all_to_all | solution.py:36
  47.9 14.7 %all_to_all.121 = bf16[64,2,32]{2,1,0:T(2,128)(2,1)S(1)} all-to-all(bf16[64,2,32]{2,1,0:T(2,128)(2,1)S(1)} %broadcast_in_dim.40), channel_id=1, replica_groups=mesh['rep_0'=8,'rep_1'=8,'rep_2'=2,'tp'=4] {'rep_0','rep_1'}, dimensions={0} | all-to-all | bytes 16384 | tf_op jit(solution)/shard_map/all_to_all | solution.py:49
  62.8 6.3 %all_to_all.122 = bf16[2,2,2048]{2,1,0:T(2,128)(2,1)S(1)} all-to-all(bf16[2,2,2048]{2,1,0:T(2,128)(2,1)S(1)} %reshape.61), channel_id=1, replica_groups=mesh['rep_0'=8,'rep_1'=8,'rep_2'=2,'tp'=4] {'rep_2'}, dimensions={0} | all-to-all | bytes 32768 | tf_op jit(solution)/shard_map/all_to_all | solution.py:49
  70.0 3.3 %all-to-all-start.5 = ((bf16[4,256,32]{1,2,0:T(8,128)(2,1)}), bf16[4,256,32]{1,2,0:T(8,128)(2,1)S(1)}, u32[]{:S(2)}, u32[]{:S(2)}) async-start(bf16[4,256,32]{1,2,0:T(8,128)(2,1)} %broadcast_in_dim.42), calls=%async_computation.5 | async-start | bytes 131072 | tf_op jit(solution)/shard_map/all_to_all | solution.py:49
  74.7 1.8 dot_general.26
  78.0 2.9 %cholesky.44 = f32[32,32]{1,0:T(8,128)S(1)} custom-call(f32[32,32]{1,0:T(8,128)S(1)} %fusion.15), custom_call_target="Cholesky" | custom-call | tf_op jit(solution)/shard_map/jit(cholesky)/cholesky | solution.py:100
  82.2 2.4 custom-call.6
  85.0 2.0 fusion.22
  87.2 4.9 %all_to_all.123 = f32[2,1,4096]{2,1,0:T(1,128)S(1)} all-to-all(f32[2,1,4096]{2,1,0:T(1,128)S(1)} %reshape.63), channel_id=1, replica_groups=mesh['rep_0'=8,'rep_1'=8,'rep_2'=2,'tp'=4] {'rep_2'}, dimensions={0} | all-to-all | bytes 65536 | tf_op jit(solution)/shard_map/all_to_all | solution.py:28
  93.0 14.9 %all_to_all.124 = f32[64,2,32]{2,1,0:T(2,128)S(1)} all-to-all(f32[64,2,32]{2,1,0:T(2,128)S(1)} %copy.110), channel_id=1, replica_groups=mesh['rep_0'=8,'rep_1'=8,'rep_2'=2,'tp'=4] {'rep_0','rep_1'}, dimensions={0} | all-to-all | bytes 32768 | tf_op jit(solution)/shard_map/all_to_all | solution.py:36
  108.0 14.9 %all_to_all.125 = f32[64,2,32]{2,1,0:T(2,128)S(1)} all-to-all(f32[64,2,32]{2,1,0:T(2,128)S(1)} %broadcast_in_dim.43), channel_id=1, replica_groups=mesh['rep_0'=8,'rep_1'=8,'rep_2'=2,'tp'=4] {'rep_0','rep_1'}, dimensions={0} | all-to-all | bytes 32768 | tf_op jit(solution)/shard_map/all_to_all | solution.py:49
  123.1 6.0 %all_to_all.126 = f32[2,1,4096]{2,1,0:T(1,128)S(1)} all-to-all(f32[2,1,4096]{2,1,0:T(1,128)S(1)} %reshape.65), channel_id=1, replica_groups=mesh['rep_0'=8,'rep_1'=8,'rep_2'=2,'tp'=4] {'rep_2'}, dimensions={0} | all-to-all | bytes 65536 | tf_op jit(solution)/shard_map/all_to_all | solution.py:49
  131.3 6.8 %all_to_all.127 = bf16[4,256,32]{1,2,0:T(8,128)(2,1)S(1)} all-to-all(bf16[4,256,32]{1,2,0:T(8,128)(2,1)S(1)} %bitcast.136), channel_id=1, replica_groups=mesh['rep_0'=8,'rep_1'=8,'rep_2'=2,'tp'=4] {'tp'}, dimensions={0} | all-to-all | bytes 131072 | tf_op jit(solution)/shard_map/all_to_all | solution.py:22
  138.5 4.9 %all_to_all.128 = f32[2,1,4096]{2,1,0:T(1,128)S(1)} all-to-all(f32[2,1,4096]{2,1,0:T(1,128)S(1)} %reshape.67), channel_id=1, replica_groups=mesh['rep_0'=8,'rep_1'=8,'rep_2'=2,'tp'=4] {'rep_2'}, dimensions={0} | all-to-all | bytes 65536 | tf_op jit(solution)/shard_map/all_to_all | solution.py:28
  144.3 15.1 %all_to_all.129 = f32[64,2,32]{2,1,0:T(2,128)S(1)} all-to-all(f32[64,2,32]{2,1,0:T(2,128)S(1)} %copy.117), channel_id=1, replica_groups=mesh['rep_0'=8,'rep_1'=8,'rep_2'=2,'tp'=4] {'rep_0','rep_1'}, dimensions={0} | all-to-all | bytes 32768 | tf_op jit(solution)/shard_map/all_to_all | solution.py:36
  159.5 14.7 %all_to_all.130 = bf16[64,2,32]{2,1,0:T(2,128)(2,1)S(1)} all-to-all(bf16[64,2,32]{2,1,0:T(2,128)(2,1)S(1)} %broadcast_in_dim.45), channel_id=1, replica_groups=mesh['rep_0'=8,'rep_1'=8,'rep_2'=2,'tp'=4] {'rep_0','rep_1'}, dimensions={0} | all-to-all | bytes 16384 | tf_op jit(solution)/shard_map/all_to_all | solution.py:49
  174.3 6.1 %all_to_all.131 = bf16[2,2,2048]{2,1,0:T(2,128)(2,1)S(1)} all-to-all(bf16[2,2,2048]{2,1,0:T(2,128)(2,1)S(1)} %reshape.69), channel_id=1, replica_groups=mesh['rep_0'=8,'rep_1'=8,'rep_2'=2,'tp'=4] {'rep_2'}, dimensions={0} | all-to-all | bytes 32768 | tf_op jit(solution)/shard_map/all_to_all | solution.py:49
  181.3 3.4 %all-to-all-start.15 = ((bf16[4,256,32]{1,2,0:T(8,128)(2,1)}), bf16[4,256,32]{1,2,0:T(8,128)(2,1)S(1)}, u32[]{:S(2)}, u32[]{:S(2)}) async-start(bf16[4,256,32]{1,2,0:T(8,128)(2,1)} %broadcast_in_dim.47), calls=%async_computation.15 | async-start | bytes 131072 | tf_op jit(solution)/shard_map/all_to_all | solution.py:49
  184.8 4.4 %all-to-all-done.15 = bf16[4,256,32]{1,2,0:T(8,128)(2,1)S(1)} async-done(((bf16[4,256,32]{1,2,0:T(8,128)(2,1)}), bf16[4,256,32]{1,2,0:T(8,128)(2,1)S(1)}, u32[]{:S(2)}, u32[]{:S(2)}) %all-to-all-start.15) | async-done | bytes 65568 | tf_op jit(solution)/shard_map/all_to_all | solution.py:49
  189.4 2.9 %cholesky.55 = f32[32,32]{1,0:T(8,128)S(1)} custom-call(f32[32,32]{1,0:T(8,128)S(1)} %fusion.13), custom_call_target="Cholesky" | custom-call | tf_op jit(solution)/shard_map/jit(cholesky)/cholesky | solution.py:100
  193.7 2.4 custom-call.7
  198.6 4.9 %all_to_all.132 = f32[2,64,84]{2,1,0:T(8,128)S(1)} all-to-all(f32[2,64,84]{2,1,0:T(8,128)S(1)} %copy.124), channel_id=1, replica_groups=mesh['rep_0'=8,'rep_1'=8,'rep_2'=2,'tp'=4] {'rep_2'}, dimensions={0} | all-to-all | bytes 86016 | tf_op jit(solution)/shard_map/all_to_all | solution.py:28
  203.5 14.7 %all_to_all.133 = f32[64,1,84]{2,1,0:T(1,128)S(1)} all-to-all(f32[64,1,84]{2,1,0:T(1,128)S(1)} %bitcast.139), channel_id=1, replica_groups=mesh['rep_0'=8,'rep_1'=8,'rep_2'=2,'tp'=4] {'rep_0','rep_1'}, dimensions={0} | all-to-all | bytes 43008 | tf_op jit(solution)/shard_map/all_to_all | solution.py:36
  218.9 4.6 %all-to-all-start.18 = ((f32[64,1,84]{2,1,0:T(1,128)}), f32[64,1,84]{2,1,0:T(1,128)S(1)}, u32[]{:S(2)}, u32[]{:S(2)}) async-start(f32[64,1,84]{2,1,0:T(1,128)} %broadcast_in_dim.48), calls=%async_computation.18 | async-start | bytes 65536 | tf_op jit(solution)/shard_map/all_to_all | solution.py:49
  223.5 10.8 %all-to-all-done.18 = f32[64,1,84]{2,1,0:T(1,128)S(1)} async-done(((f32[64,1,84]{2,1,0:T(1,128)}), f32[64,1,84]{2,1,0:T(1,128)S(1)}, u32[]{:S(2)}, u32[]{:S(2)}) %all-to-all-start.18) | async-done | bytes 21536 | tf_op jit(solution)/shard_map/all_to_all | solution.py:49
  234.3 6.1 %all_to_all.134 = f32[2,64,84]{2,1,0:T(8,128)S(1)} all-to-all(f32[2,64,84]{2,1,0:T(8,128)S(1)} %broadcast_in_dim.49), channel_id=1, replica_groups=mesh['rep_0'=8,'rep_1'=8,'rep_2'=2,'tp'=4] {'rep_2'}, dimensions={0} | all-to-all | bytes 86016 | tf_op jit(solution)/shard_map/all_to_all | solution.py:49
  243.2 4.8 %all-to-all-start.20 = ((bf16[64,8,256]{2,1,0:T(8,128)(2,1)}), bf16[64,8,256]{2,1,0:T(8,128)(2,1)S(1)}, u32[]{:S(2)}, u32[]{:S(2)}) async-start(bf16[64,8,256]{2,1,0:T(8,128)(2,1)} %broadcast_in_dim.51), calls=%async_computation.20 | async-start | bytes 524288 | tf_op jit(solution)/shard_map/all_to_all | solution.py:49
  249.7 11.7 %all-to-all-done.20 = bf16[64,8,256]{2,1,0:T(8,128)(2,1)S(1)} async-done(((bf16[64,8,256]{2,1,0:T(8,128)(2,1)}), bf16[64,8,256]{2,1,0:T(8,128)(2,1)S(1)}, u32[]{:S(2)}, u32[]{:S(2)}) %all-to-all-start.20) | async-done | bytes 262176 | tf_op jit(solution)/shard_map/all_to_all | solution.py:49
  261.4 6.0 %all_to_all.135 = bf16[2,64,8,256]{3,2,1,0:T(8,128)(2,1)S(1)} all-to-all(bf16[2,64,8,256]{3,2,1,0:T(8,128)(2,1)S(1)} %broadcast_in_dim.52), channel_id=1, replica_groups=mesh['rep_0'=8,'rep_1'=8,'rep_2'=2,'tp'=4] {'rep_2'}, dimensions={0} | all-to-all | bytes 1048576 | tf_op jit(solution)/shard_map/all_to_all | solution.py:49
  (111 shorter events, 24.2 us)
Async XLA Ops:
  0.6 0.8 copy-start
  3.9 69.4 %copy-start.1 = (f32[1,1024,256]{2,1,0:T(8,128)S(1)}, f32[1,1024,256]{2,1,0:T(8,128)}, u32[]{:S(2)}) copy-start(f32[1,1024,256]{2,1,0:T(8,128)} %param.12) | copy-start | bytes 3145732
  23.9 49.4 %copy-start.2 = (bf16[1,1024,256]{2,1,0:T(8,128)(2,1)S(1)}, bf16[1,1024,256]{2,1,0:T(8,128)(2,1)}, u32[]{:S(2)}) copy-start(bf16[1,1024,256]{2,1,0:T(8,128)(2,1)} %param.11) | copy-start | bytes 1572868
  70.0 7.7 %all-to-all-start.5 = ((bf16[4,256,32]{1,2,0:T(8,128)(2,1)}), bf16[4,256,32]{1,2,0:T(8,128)(2,1)S(1)}, u32[]{:S(2)}, u32[]{:S(2)}) async-start(bf16[4,256,32]{1,2,0:T(8,128)(2,1)} %broadcast_in_dim.42), calls=%async_computation.5 | async-start | bytes 131072 | tf_op jit(solution)/shard_map/all_to_all | solution.py:49
  181.3 3.4 %copy-start.5 = (f32[1,2560]{1,0:T(1,128)S(1)}, f32[1,2560]{1,0:T(1,128)}, u32[]{:S(2)}) copy-start(f32[1,2560]{1,0:T(1,128)} %param.16) | copy-start | bytes 30724
  181.3 7.9 %all-to-all-start.15 = ((bf16[4,256,32]{1,2,0:T(8,128)(2,1)}), bf16[4,256,32]{1,2,0:T(8,128)(2,1)S(1)}, u32[]{:S(2)}, u32[]{:S(2)}) async-start(bf16[4,256,32]{1,2,0:T(8,128)(2,1)} %broadcast_in_dim.47), calls=%async_computation.15 | async-start | bytes 131072 | tf_op jit(solution)/shard_map/all_to_all | solution.py:49
  218.9 15.4 %all-to-all-start.18 = ((f32[64,1,84]{2,1,0:T(1,128)}), f32[64,1,84]{2,1,0:T(1,128)S(1)}, u32[]{:S(2)}, u32[]{:S(2)}) async-start(f32[64,1,84]{2,1,0:T(1,128)} %broadcast_in_dim.48), calls=%async_computation.18 | async-start | bytes 65536 | tf_op jit(solution)/shard_map/all_to_all | solution.py:49
  240.8 1.1 copy-start.6
  240.8 1.1 copy-start.7
  243.2 4.8 %copy-start.3 = (f32[2560]{0:T(1024)S(1)}, f32[2560]{0:T(1024)}, u32[]{:S(2)}) copy-start(f32[2560]{0:T(1024)} %param.17) | copy-start | bytes 30724
  243.2 4.8 %copy-start.4 = (f32[2560]{0:T(1024)S(1)}, f32[2560]{0:T(1024)}, u32[]{:S(2)}) copy-start(f32[2560]{0:T(1024)} %param.18) | copy-start | bytes 30724
  243.2 18.2 %all-to-all-start.20 = ((bf16[64,8,256]{2,1,0:T(8,128)(2,1)}), bf16[64,8,256]{2,1,0:T(8,128)(2,1)S(1)}, u32[]{:S(2)}, u32[]{:S(2)}) async-start(bf16[64,8,256]{2,1,0:T(8,128)(2,1)} %broadcast_in_dim.51), calls=%async_computation.20 | async-start | bytes 524288 | tf_op jit(solution)/shard_map/all_to_all | solution.py:49
where the time goes:
time: 270 us; the launch traced here: 268 us
  blocking collectives  183 us (68%)
  waiting for transfers between devices  28 us (10%)
  other arithmetic  19.3 us (7%)
  starting transfers between devices  16 us (6%)
  local copies, waits for them, and re-layouts  11.5 us (4%)
  matrix products  9.32 us (3%)
    all_to_all x8, blocking collectives, sent_to_all(): return lax.all_to_all(copies, axis, split_axis=0, concat_axis=0, tiled=True)  74.7 us
    all_to_all x4, blocking collectives, sum_by_axis(): lax.all_to_all(nearer, far, split_axis=0, concat_axis=0, tiled=True)  68.4 us
    all_to_all x4, waiting for transfers between devices, sent_to_all(): return lax.all_to_all(copies, axis, split_axis=0, concat_axis=0, tiled=True)  28 us
    all_to_all x4, blocking collectives, sent_and_summed_2(): lax.all_to_all(in_blocks(array, dim, peers), axis, 0, 0, tiled=True)  23.8 us
    all_to_all x2, blocking collectives, sent_and_summed(): lax.all_to_all(in_blocks(array, dim, peers), axis, 0, 0, tiled=True)  16.1 us
    all_to_all x4, starting transfers between devices, sent_to_all(): return lax.all_to_all(copies, axis, split_axis=0, concat_axis=0, tiled=True)  16 us
    another operation x6, other arithmetic, orthonormal(): lower = jnp.linalg.cholesky(gram)  7.2 us
    another operation x4, other arithmetic, orthonormal(): return jax.scipy.linalg.solve_triangular(lower, left.T, lower=True).T  6.17 us
  transfers between devices with their start and end apart: 4, of which 4 were waited for; matrix products, arithmetic and copies ran while one was open for 2% of the time, Pallas kernels for 0%

commit v1 on v0

v1 whole, which is shorter than its diff:
```python
import jax
import jax.numpy as jnp
from jax import lax
from jax.sharding import Mesh
from jax.sharding import PartitionSpec as P

REP = ("y", "z", "c")
CHIPS = ("y", "z")
PRECISE = lax.Precision.HIGHEST
MOMENTUM_RATE = 0.9
LEARN_RATE = 0.5
F32 = jnp.float32
BF16 = jnp.bfloat16
SWAP = ((0, 1), (1, 0))


def split(values):
    high = values.astype(BF16)
    return high, (values - high.astype(F32)).astype(BF16)


def exchange(array, axis):
    return lax.all_to_all(array, axis, 0, 0, tiled=True)


def sent_to_all(array, axis):
    peers = lax.axis_size(axis)
    return exchange(jnp.broadcast_to(array, (peers, *array.shape)), axis)


def factor_of(left):
    return jnp.linalg.cholesky(jnp.dot(left.T, left, precision=PRECISE))


def solved(lower, left):
    return jax.scipy.linalg.solve_triangular(lower, left.T, lower=True).T


def shards(
    gradients,
    feedback,
    warm_factor,
    momentum,
    master_owned,
    vector_grads,
    vector_params,
    vector_momentum,
):
    replicas = lax.axis_size(REP)
    chips = lax.axis_size(CHIPS)
    core = lax.axis_index("c")
    rows, cols = gradients.shape[1:]
    owned = momentum.shape[0]
    rank = warm_factor.shape[1]
    combined = gradients[0].astype(F32) + feedback[0]

    by_owner = combined.reshape(chips, 2, owned, cols)
    part = vector_grads.shape[1] // replicas
    vector_parts = vector_grads.reshape(2, chips, 1, part)
    lanes = 128

    def packed(side):
        block = lax.dynamic_index_in_dim(by_owner, side, 1, keepdims=False)
        values = lax.dynamic_index_in_dim(vector_parts, side, 0, keepdims=False)
        high, low = split(values)
        extra = jnp.concatenate([high, low], 1).astype(F32)
        extra = jnp.pad(extra, ((0, 0), (0, owned - 2), (0, lanes - part)))
        return jnp.concatenate([block, extra], 2)

    other = lax.ppermute(packed(1 - core).astype(BF16), "c", SWAP)
    paired = packed(core) + other.astype(F32)
    pair_vector = paired[:, 0, cols : cols + part] + paired[:, 1, cols : cols + part]
    high, low = split(pair_vector)
    sending = jnp.concatenate([paired[:, :, :cols].astype(BF16), jnp.pad(jnp.stack([high, low], 1), ((0, 0), (0, owned - 2), (0, lanes - part)))], 2)
    arrived = exchange(sending, CHIPS).astype(F32).sum(0)
    block = arrived[:, :cols]
    own_vector = arrived[0, cols : cols + part] + arrived[1, cols : cols + part]

    left_rows = jnp.dot(block, warm_factor, precision=PRECISE)
    left_rows = sent_to_all(left_rows, "tp").sum(0)

    base = master_owned - LEARN_RATE * MOMENTUM_RATE * momentum
    left_high, left_low = split(left_rows)
    high, low = split(own_vector)
    vector_lanes = jnp.pad(jnp.stack([high, low], 0), ((0, owned - 2), (0, lanes - 2 * rank - part)))
    shared = jnp.concatenate([block.astype(BF16), left_high, left_low, vector_lanes, base.astype(BF16)], 1)
    near = sent_to_all(shared, CHIPS)
    far = lax.ppermute(near, "c", SWAP)
    whole = jnp.where(core == 0, jnp.stack([near, far], 1), jnp.stack([far, near], 1))
    flat = whole.reshape(rows, -1)
    summed = flat[:, :cols].astype(F32)
    left_one = flat[:, cols : cols + rank].astype(F32) + flat[:, cols + rank : cols + 2 * rank].astype(F32)
    base_rows = flat[:, cols + lanes :].astype(F32)
    at = cols + 2 * rank
    vector_sum = (whole[:, :, 0, at : at + part].astype(F32) + whole[:, :, 1, at : at + part].astype(F32)).swapaxes(0, 1).reshape(-1)

    right = lax.dot_general(summed, left_one, (((0,), (0,)), ((), ())), precision=PRECISE)
    partial = jnp.dot(summed, right, precision=PRECISE).astype(BF16)
    lower_one = factor_of(left_one)
    left_two = sent_to_all(partial, "tp").astype(F32).sum(0)
    left_two = solved(lower_one, left_two)
    ortho_two = solved(factor_of(left_two), left_two)
    right_two = lax.dot_general(summed, ortho_two, (((0,), (0,)), ((), ())), precision=PRECISE)
    approx = jnp.dot(ortho_two, right_two.T, precision=PRECISE) / replicas

    new_feedback = (combined - approx)[None]
    row_start = lax.axis_index(REP) * owned
    owned_approx = lax.dynamic_slice_in_dim(approx, row_start, owned, 0)
    new_momentum = MOMENTUM_RATE * momentum + owned_approx
    new_master = master_owned - LEARN_RATE * new_momentum
    weight = (base_rows - LEARN_RATE * approx).astype(BF16)
    new_vector_momentum = MOMENTUM_RATE * vector_momentum + vector_sum / replicas
    new_vector_params = vector_params - LEARN_RATE * new_vector_momentum
    return (new_feedback, new_momentum, new_master, weight, new_vector_params, new_vector_momentum)


def solution(mesh):
    finer = Mesh(mesh.devices.reshape(8, 8, 2, mesh.shape["tp"]), ("y", "z", "c", "tp"))
    in_specs = (
        P(REP, None, "tp"),
        P(REP, None, "tp"),
        P("tp", None),
        P(REP, "tp"),
        P(REP, "tp"),
        P(REP, None),
        P(),
        P(),
    )
    out_specs = (P(REP, None, "tp"), P(REP, "tp"), P(REP, "tp"), P(None, "tp"), P(), P())
    return jax.shard_map(
        shards, mesh=finer, in_specs=in_specs, out_specs=out_specs, check_vma=False
    )
```

time: 270 us -> 116 us (0.43)
  blocking collectives: 183 us -> 23.5 us
  starting transfers between devices: 16 us -> 34.6 us
  local copies, waits for them, and re-layouts: 11.5 us -> 3.19 us
  matrix products: 9.32 us -> 6 us
    all_to_all x18 -> x1, blocking collectives: 183 us -> 23.5 us  [exchange(): return lax.all_to_all(array, axis, 0, 0, tiled=True)]
    ppermute x0 -> x2, starting transfers between devices: none -> 16.2 us  [the longest x1 8.75 us: shards(): other = lax.ppermute(packed(1 - core).astype(BF16), 'c', SWAP)]
    dot_general x6, matrix products: 7.66 us -> 3.11 us  [the longest x2 1.38 us: factor_of(): return jnp.linalg.cholesky(jnp.dot(left.T, left, precision=PRECISE))]
    all_to_all x4 -> x3, waiting for transfers between devices: 28 us -> 24.5 us  [exchange(): return lax.all_to_all(array, axis, 0, 0, tiled=True)]
    dot_general x4 -> x2, local copies, waits for them, and re-layouts: 3.3 us -> 0.14 us  [factor_of(): return jnp.linalg.cholesky(jnp.dot(left.T, left, precision=PRECISE))]
    all_to_all x4 -> x3, starting transfers between devices: 16 us -> 18.4 us  [exchange(): return lax.all_to_all(array, axis, 0, 0, tiled=True)]
    another operation x10 -> x12, other arithmetic: 13.4 us -> 13.5 us  [the longest x6 7.19 us: factor_of(): return jnp.linalg.cholesky(jnp.dot(left.T, left, precision=PRECISE))]
  transfers between devices with their start and end apart: 4 -> 5, of which waited for: 4 -> 5; matrix products, arithmetic and copies ran while one was open for 2% -> 1% of each run, Pallas kernels for 0% -> 0%
where the time goes in v1:
time: 116 us; the launch traced here: 115 us
  starting transfers between devices  34.6 us (30%)
  waiting for transfers between devices  27.1 us (23%)
  blocking collectives  23.5 us (20%)
  other arithmetic  19.3 us (17%)
  matrix products  6 us (5%)
  local copies, waits for them, and re-layouts  3.19 us (3%)
    all_to_all x3, waiting for transfers between devices, exchange(): return lax.all_to_all(array, axis, 0, 0, tiled=True)  24.5 us
    all_to_all x1, blocking collectives, exchange(): return lax.all_to_all(array, axis, 0, 0, tiled=True)  23.5 us
    all_to_all x3, starting transfers between devices, exchange(): return lax.all_to_all(array, axis, 0, 0, tiled=True)  18.4 us
    ppermute x1, starting transfers between devices, shards(): other = lax.ppermute(packed(1 - core).astype(BF16), 'c', SWAP)  8.75 us
    ppermute x1, starting transfers between devices, shards(): far = lax.ppermute(near, 'c', SWAP)  7.5 us
    another operation x6, other arithmetic, factor_of(): return jnp.linalg.cholesky(jnp.dot(left.T, left, precision=PRECISE))  7.19 us
    another operation x4, other arithmetic, solved(): return jax.scipy.linalg.solve_triangular(lower, left.T, lower=True).T  6.17 us
  transfers between devices with their start and end apart: 5, of which 5 were waited for; matrix products, arithmetic and copies ran while one was open for 1% of the time, Pallas kernels for 0%

profile of v1, /device:TPU:1, one launch (start us, length us, event | category | flops | bytes accessed | tf_op | source)
XLA Modules:
  0.0 114.8 jit_solution(18122141999378731388)
XLA Ops:
  0.7 0.7 reduce.4
  1.8 1.5 %convert_add_fusion = f32[1,1024,256]{2,1,0:T(8,128)S(1)} fusion(f32[1,1024,256]{2,1,0:T(8,128)} %param.12, bf16[1,1024,256]{2,1,0:T(8,128)(2,1)} %param.11), kind=kLoop, calls=%fused_computation.5 | loop fusion | flops 524288 | bytes 2621440 | tf_op jit(solution)/shard_map/add | solution.py:55
  3.4 8.7 %collective-permute-start = (bf16[64,8,384]{2,1,0:T(8,128)(2,1)S(1)}, bf16[64,8,384]{2,1,0:T(8,128)(2,1)S(1)}, u32[]{:S(2)}, u32[]{:S(2)}) collective-permute-start(bf16[64,8,384]{2,1,0:T(8,128)(2,1)S(1)} %fusion.8), channel_id=1, source_target_pairs={{0,4},{4,0},{1,5},{5,1},{2,6},{6,2},{3,7},{7,3},{8,12},{12,8},{9,1... | collective-permute-start | bytes 1179656 | tf_op jit(solution)/shard_map/ppermute | solution.py:70
  12.5 1.0 collective-permute-done
  13.8 0.8 pad_maximum_fusion
  14.6 11.0 %all-to-all-start = ((bf16[64,8,384]{2,1,0:T(8,128)(2,1)}), bf16[64,8,384]{2,1,0:T(8,128)(2,1)S(1)}, u32[]{:S(2)}, u32[]{:S(2)}) async-start(bf16[64,8,384]{2,1,0:T(8,128)(2,1)} %pad_maximum_fusion), calls=%async_computation | async-start | bytes 786432 | tf_op jit(solution)/shard_map/all_to_all | solution.py:23
  25.6 14.9 %all-to-all-done = bf16[64,8,384]{2,1,0:T(8,128)(2,1)S(1)} async-done(((bf16[64,8,384]{2,1,0:T(8,128)(2,1)}), bf16[64,8,384]{2,1,0:T(8,128)(2,1)S(1)}, u32[]{:S(2)}, u32[]{:S(2)}) %all-to-all-start) | async-done | bytes 393248 | tf_op jit(solution)/shard_map/all_to_all | solution.py:23
  40.8 0.7 reshape.117
  41.5 4.0 %all-to-all-start.1 = ((f32[4,1,256]{2,1,0:T(1,128)}), f32[4,1,256]{2,1,0:T(1,128)S(1)}, u32[]{:S(2)}, u32[]{:S(2)}) async-start(f32[4,1,256]{2,1,0:T(1,128)} %reshape.117), calls=%async_computation.1 | async-start | bytes 8192 | tf_op jit(solution)/shard_map/all_to_all | solution.py:23
  45.5 4.1 %all-to-all-done.1 = f32[4,1,256]{2,1,0:T(1,128)S(1)} async-done(((f32[4,1,256]{2,1,0:T(1,128)}), f32[4,1,256]{2,1,0:T(1,128)S(1)}, u32[]{:S(2)}, u32[]{:S(2)}) %all-to-all-start.1) | async-done | bytes 4128 | tf_op jit(solution)/shard_map/all_to_all | solution.py:23
  49.6 0.5 broadcast.83
  50.1 0.7 reduce.5
  51.0 23.5 %all_to_all.20 = bf16[64,8,640]{2,1,0:T(8,128)(2,1)S(1)} all-to-all(bf16[64,8,640]{2,1,0:T(8,128)(2,1)S(1)} %broadcast_in_dim.14), channel_id=1, replica_groups=mesh['y'=8,'z'=8,'c'=2,'tp'=4] {'y','z'}, dimensions={0} | all-to-all | bytes 1310720 | tf_op jit(solution)/shard_map/all_to_all | solution.py:23
  74.6 7.5 %collective-permute-start.1 = (bf16[64,8,640]{2,1,0:T(8,128)(2,1)S(1)}, bf16[64,8,640]{2,1,0:T(8,128)(2,1)S(1)}, u32[]{:S(2)}, u32[]{:S(2)}) collective-permute-start(bf16[64,8,640]{2,1,0:T(8,128)(2,1)S(1)} %all_to_all.20), channel_id=1, source_target_pairs={{0,4},{4,0},{1,5},{5,1},{2,6},{6,2},{3,7},{7,3},{8,12},{12,8},{9,1... | collective-permute-start | bytes 1966088 | tf_op jit(solution)/shard_map/ppermute | solution.py:88
  82.1 1.7 %collective-permute-done.1 = bf16[64,8,640]{2,1,0:T(8,128)(2,1)S(1)} collective-permute-done((bf16[64,8,640]{2,1,0:T(8,128)(2,1)S(1)}, bf16[64,8,640]{2,1,0:T(8,128)(2,1)S(1)}, u32[]{:S(2)}, u32[]{:S(2)}) %collective-permute-start.1) | collective-permute-done | bytes 655392 | tf_op jit(solution)/shard_map/ppermute | solution.py:88
  84.3 1.1 fusion.3
  85.5 0.7 fusion.2
  86.3 2.9 %cholesky.44 = f32[32,32]{1,0:T(8,128)S(1)} custom-call(f32[32,32]{1,0:T(8,128)S(1)} %fusion.30), custom_call_target="Cholesky" | custom-call | tf_op jit(solution)/shard_map/jit(cholesky)/cholesky | solution.py:32
  89.3 0.6 compare_reduce_fusion.1
  89.9 0.7 fusion.24
  90.6 2.4 %custom-call.6 = f32[1,32,32]{1,2,0:T(8,128)S(1)} custom-call(f32[1,32,32]{2,1,0:T(8,128)S(1)} %fusion.24), custom_call_target="InvertDiagBlocksLowerTriangular" | custom-call | tf_op jit(solution)/shard_map/jit(_solve_triangular)/triangular_solve | solution.py:36
  93.0 0.6 convolution_convert_fusion
  93.6 0.7 broadcast_in_dim.15
  94.4 3.4 %all-to-all-start.3 = ((bf16[4,1024,32]{1,2,0:T(8,128)(2,1)}), bf16[4,1024,32]{1,2,0:T(8,128)(2,1)S(1)}, u32[]{:S(2)}, u32[]{:S(2)}) async-start(bf16[4,1024,32]{1,2,0:T(8,128)(2,1)} %broadcast_in_dim.15), calls=%async_computation.3 | async-start | bytes 524288 | tf_op jit(solution)/shard_map/all_to_all | solution.py:23
  97.8 0.6 multiply_subtract_fusion
  98.4 5.4 %all-to-all-done.3 = bf16[4,1024,32]{1,2,0:T(8,128)(2,1)S(1)} async-done(((bf16[4,1024,32]{1,2,0:T(8,128)(2,1)}), bf16[4,1024,32]{1,2,0:T(8,128)(2,1)S(1)}, u32[]{:S(2)}, u32[]{:S(2)}) %all-to-all-start.3) | async-done | bytes 262176 | tf_op jit(solution)/shard_map/all_to_all | solution.py:23
  104.5 2.9 %cholesky.55 = f32[32,32]{1,0:T(8,128)S(1)} custom-call(f32[32,32]{1,0:T(8,128)S(1)} %fusion.28), custom_call_target="Cholesky" | custom-call | tf_op jit(solution)/shard_map/jit(cholesky)/cholesky | solution.py:32
  107.5 0.6 compare_reduce_fusion
  108.1 0.7 fusion.25
  108.8 2.4 %custom-call.7 = f32[1,32,32]{1,2,0:T(8,128)S(1)} custom-call(f32[1,32,32]{2,1,0:T(8,128)S(1)} %fusion.25), custom_call_target="InvertDiagBlocksLowerTriangular" | custom-call | tf_op jit(solution)/shard_map/jit(_solve_triangular)/triangular_solve | solution.py:36
  111.9 2.2 %subtract_convert_fusion = (bf16[1024,256]{1,0:T(8,128)(2,1)}, f32[1,1024,256]{2,1,0:T(8,128)}, f32[1024,256]{1,0:T(8,128)S(1)}) fusion(bf16[1024,640]{1,0:T(8,128)(2,1)S(1)} %bitcast.70, f32[1,1024,256]{2,1,0:T(8,128)S(1)} %convert_add_fusion, f32[32,1024]{1,0:T(8,128)S(1)} %fusion.26, f32[256,32]{0,1:T(8,128)S(1)} %fusion.4), kind=kOutput, calls=%fused_computation.4 | convolution fusion | flops 102236160 | bytes 4358144 | tf_op jit(solution)/shard_map/dot_general | solution.py:104
  114.2 0.6 multiply_subtract_fusion.1
  (57 shorter events, 3.8 us)
Async XLA Ops:
  0.6 40.0 %copy-start = (f32[256,32]{0,1:T(8,128)S(1)}, f32[256,32]{0,1:T(8,128)}, u32[]{:S(2)}) copy-start(f32[256,32]{0,1:T(8,128)} %param.13) | copy-start | bytes 98308
  3.4 10.1 %collective-permute-start = (bf16[64,8,384]{2,1,0:T(8,128)(2,1)S(1)}, bf16[64,8,384]{2,1,0:T(8,128)(2,1)S(1)}, u32[]{:S(2)}, u32[]{:S(2)}) collective-permute-start(bf16[64,8,384]{2,1,0:T(8,128)(2,1)S(1)} %fusion.8), channel_id=1, source_target_pairs={{0,4},{4,0},{1,5},{5,1},{2,6},{6,2},{3,7},{7,3},{8,12},{12,8},{9,1... | collective-permute-start | bytes 1179656 | tf_op jit(solution)/shard_map/ppermute | solution.py:70
  13.5 12.0 %copy-start.1 = (f32[8,256]{1,0:T(8,128)S(1)}, f32[8,256]{1,0:T(8,128)}, u32[]{:S(2)}) copy-start(f32[8,256]{1,0:T(8,128)} %param.15) | copy-start | bytes 24580
  13.5 12.0 %copy-start.2 = (f32[8,256]{1,0:T(8,128)S(1)}, f32[8,256]{1,0:T(8,128)}, u32[]{:S(2)}) copy-start(f32[8,256]{1,0:T(8,128)} %param.14) | copy-start | bytes 24580
  14.6 25.9 %all-to-all-start = ((bf16[64,8,384]{2,1,0:T(8,128)(2,1)}), bf16[64,8,384]{2,1,0:T(8,128)(2,1)S(1)}, u32[]{:S(2)}, u32[]{:S(2)}) async-start(bf16[64,8,384]{2,1,0:T(8,128)(2,1)} %pad_maximum_fusion), calls=%async_computation | async-start | bytes 786432 | tf_op jit(solution)/shard_map/all_to_all | solution.py:23
  41.5 8.2 %all-to-all-start.1 = ((f32[4,1,256]{2,1,0:T(1,128)}), f32[4,1,256]{2,1,0:T(1,128)S(1)}, u32[]{:S(2)}, u32[]{:S(2)}) async-start(f32[4,1,256]{2,1,0:T(1,128)} %reshape.117), calls=%async_computation.1 | async-start | bytes 8192 | tf_op jit(solution)/shard_map/all_to_all | solution.py:23
  74.6 9.2 %collective-permute-start.1 = (bf16[64,8,640]{2,1,0:T(8,128)(2,1)S(1)}, bf16[64,8,640]{2,1,0:T(8,128)(2,1)S(1)}, u32[]{:S(2)}, u32[]{:S(2)}) collective-permute-start(bf16[64,8,640]{2,1,0:T(8,128)(2,1)S(1)} %all_to_all.20), channel_id=1, source_target_pairs={{0,4},{4,0},{1,5},{5,1},{2,6},{6,2},{3,7},{7,3},{8,12},{12,8},{9,1... | collective-permute-start | bytes 1966088 | tf_op jit(solution)/shard_map/ppermute | solution.py:88
  85.5 12.3 %copy-start.3 = (f32[2560]{0:T(1024)S(1)}, f32[2560]{0:T(1024)}, u32[]{:S(2)}) copy-start(f32[2560]{0:T(1024)} %param.17) | copy-start | bytes 30724
  85.5 12.3 %copy-start.4 = (f32[2560]{0:T(1024)S(1)}, f32[2560]{0:T(1024)}, u32[]{:S(2)}) copy-start(f32[2560]{0:T(1024)} %param.18) | copy-start | bytes 30724
  94.4 9.5 %all-to-all-start.3 = ((bf16[4,1024,32]{1,2,0:T(8,128)(2,1)}), bf16[4,1024,32]{1,2,0:T(8,128)(2,1)S(1)}, u32[]{:S(2)}, u32[]{:S(2)}) async-start(bf16[4,1024,32]{1,2,0:T(8,128)(2,1)} %broadcast_in_dim.15), calls=%async_computation.3 | async-start | bytes 524288 | tf_op jit(solution)/shard_map/all_to_all | solution.py:23

commit v2 on v1

v2 whole, which is shorter than its diff:
```python
import functools

import jax
import jax.numpy as jnp
from jax import lax
from jax.experimental import pallas as pl
from jax.experimental.pallas import tpu as pltpu
from jax.sharding import Mesh
from jax.sharding import PartitionSpec as P

REP = ("y", "z", "c")
CHIPS = ("y", "z")
PRECISE = lax.Precision.HIGHEST
MOMENTUM_RATE = 0.9
LEARN_RATE = 0.5
F32 = jnp.float32
BF16 = jnp.bfloat16
SWAP = ((0, 1), (1, 0))
LANES = 128
PIVOTS = 8
CHUNKS = 4
VMEM = pl.BlockSpec(memory_space=pltpu.VMEM)
SMEM = pl.BlockSpec(memory_space=pltpu.SMEM)
ANY = pl.BlockSpec(memory_space=pl.ANY)
SMALL = pltpu.CompilerParams(vmem_limit_bytes=8 << 20)
LARGE = pltpu.CompilerParams(vmem_limit_bytes=20 << 20)


def split(values):
    high = values.astype(BF16)
    return high, (values - high.astype(F32)).astype(BF16)


def exchange(array, axis):
    return lax.all_to_all(array, axis, 0, 0, tiled=True)


def product(left, right, dims, precision=None):
    return lax.dot_general(left, right, (dims, ((), ())), precision=precision, preferred_element_type=F32)


def times_exact(factor, exact, dims):
    both = product(jnp.concatenate(split(factor), 0), exact, dims)
    rows = factor.shape[0]
    return both[:rows] + both[rows:]


def lower_inverse(gram):
    n = gram.shape[0]
    lane = lax.broadcasted_iota(jnp.int32, (n, LANES), 1)
    row = lax.broadcasted_iota(jnp.int32, (n, LANES), 0)
    eye = jnp.where(lane == row + n, 1.0, 0.0).astype(F32)
    work = jnp.concatenate([gram, jnp.zeros((n, LANES - n), F32)], 1) + eye
    inverses = []
    for first in range(0, n, PIVOTS):
        cols = [jnp.broadcast_to(work[:, first + j : first + j + 1], (n, LANES)) for j in range(PIVOTS)]
        lines = [work[first + j : first + j + 1, :] for j in range(PIVOTS)]
        for j in range(PIVOTS):
            at = first + j
            inverse = 1.0 / cols[j][at : at + 1, :]
            inverses.append(inverse)
            scaled = lines[j] * inverse
            below = jnp.where(row > at, cols[j], 0.0)
            for m in range(j + 1, PIVOTS):
                lines[m] = lines[m] - cols[j][first + m : first + m + 1, :] * scaled
                cols[m] = cols[m] - below * (cols[m][at : at + 1, :] * inverse)
            work = work - below * scaled
    return (work * jnp.sqrt(jnp.concatenate(inverses, 0)))[:, n : 2 * n]


def gram_inverse(left):
    return lower_inverse(product(left, left, ((1,), (1,)), PRECISE))


def share_kernel(arrived, momentum, master, out):
    cols = momentum.shape[1]
    total = jnp.sum(arrived[...].astype(F32), axis=0)
    high, low = split(total[0:1, cols:] + total[1:2, cols:])
    row = lax.broadcasted_iota(jnp.int32, (total.shape[0], LANES), 0)
    vector = jnp.where(row == 0, high.astype(F32), jnp.where(row == 1, low.astype(F32), 0.0))
    base = master[...] - LEARN_RATE * MOMENTUM_RATE * momentum[...]
    shared = jnp.concatenate([total[:, :cols], vector, base], 1).astype(BF16)
    out[...] = jnp.broadcast_to(shared, out.shape)


def matrix_of(ref, cols):
    return ref[:, :, :cols].reshape(-1, cols)


def left_kernel(near, factor, out):
    cols = factor.shape[0]
    left = times_exact(factor[...].T, matrix_of(near, cols), ((1,), (1,)))
    out[...] = jnp.broadcast_to(left.astype(BF16), out.shape)


def left_sum(place, arrived):
    tp = arrived.shape[0] // 2
    core = place[0]

    def half(side):
        return jnp.sum(arrived[pl.ds(side * tp, tp)].astype(F32), axis=0)

    return half(core), half(1 - core)


def power_kernel(place, arrived, near, far, out, vector):
    cols = near.shape[2] * 2 // 5
    core = place[0]
    for side, ref in ((core, near), (1 - core, far)):
        vector[side] = ref[:, 0, cols : cols + LANES].astype(F32) + ref[:, 1, cols : cols + LANES].astype(F32)
    own, other = left_sum(place, arrived)
    near_matrix, far_matrix = matrix_of(near, cols), matrix_of(far, cols)
    right = times_exact(own, near_matrix, ((1,), (0,))) + times_exact(other, far_matrix, ((1,), (0,)))
    half = own.shape[1]
    for side, matrix in enumerate((near_matrix, far_matrix)):
        left = times_exact(right, matrix, ((1,), (1,))).astype(BF16)
        out[:, :, side * half : (side + 1) * half] = jnp.broadcast_to(left, (out.shape[0], *left.shape))


def factor_kernel(place, arrived, after, out):
    del after
    own, other = left_sum(place, arrived)
    out[...] = gram_inverse(jnp.concatenate([own, other], 1))


def finish_kernel(
    place,
    parts,
    inverse_one,
    near,
    far,
    gradients,
    feedback,
    momentum,
    master,
    new_feedback,
    weight,
    new_momentum,
    new_master,
    ortho_terms,
    right_terms,
    feedback_buffer,
    weight_buffer,
    base,
    owned,
    sems,
    *,
    replicas,
):
    core, chip = place[0], place[1]
    chips, pair, cols = feedback.shape
    rows = pair // 2
    half = chips * rows
    for side, ref in ((core, near), (1 - core, far)):
        base[side] = ref[:, :, cols + LANES :]
    left = product(inverse_one[...], jnp.sum(parts[...].astype(F32), axis=0), ((1,), (0,)), PRECISE)
    ortho = product(gram_inverse(left), left, ((1,), (0,)), PRECISE)
    right = times_exact(ortho[:, :half], matrix_of(near, cols), ((1,), (0,)))
    right += times_exact(ortho[:, half:], matrix_of(far, cols), ((1,), (0,)))
    right_high, right_low = split(right / replicas)
    right_terms[...] = jnp.concatenate([right_high, right_low, right_high], 0)
    for side, start in enumerate((core * half, (1 - core) * half)):
        high, low = split(ortho[:, side * half : (side + 1) * half])
        ortho_terms[:, pl.ds(pl.multiple_of(start, LANES), half)] = jnp.concatenate([high, high, low], 0)
    step = chips // CHUNKS
    copies = []
    for chunk in range(CHUNKS):
        span = slice(chunk * step, (chunk + 1) * step)
        sides = []
        for side in range(2):
            at = side * half + chunk * step * rows
            terms = ortho_terms[:, at : at + step * rows]
            sides.append(product(terms, right_terms[...], ((0,), (0,))).reshape(step, rows, cols))
        approx = jnp.concatenate(sides, 1)
        owned[:, span] = jnp.stack(sides, 0)
        feedback_buffer[span] = gradients[span].astype(F32) + feedback[span] - approx
        kept = [base[side, span].astype(F32) for side in range(2)]
        weight_buffer[span] = (jnp.concatenate(kept, 1) - LEARN_RATE * approx).astype(BF16)
        for which, (source, target) in enumerate(((feedback_buffer, new_feedback), (weight_buffer, weight))):
            copy = pltpu.make_async_copy(source.at[span], target.at[span], sems.at[chunk, which])
            copy.start()
            copies.append(copy)
    moved = MOMENTUM_RATE * momentum[...] + owned[core, chip]
    new_momentum[...] = moved
    new_master[...] = master[...] - LEARN_RATE * moved
    for copy in copies:
        copy.wait()


def shards(
    gradients,
    feedback,
    warm_factor,
    momentum,
    master_owned,
    vector_grads,
    vector_params,
    vector_momentum,
):
    replicas = lax.axis_size(REP)
    chips = lax.axis_size(CHIPS)
    tp = lax.axis_size("tp")
    core = lax.axis_index("c")
    rows, cols = gradients.shape[1:]
    owned = momentum.shape[0]
    rank = warm_factor.shape[1]
    half = rows // 2
    place = jnp.stack([core, lax.axis_index(CHIPS)]).astype(jnp.int32)
    by_pair = (chips, 2 * owned, cols)

    combined = gradients[0].astype(F32) + feedback[0]
    by_owner = combined.reshape(chips, 2, owned, cols)
    part = vector_grads.shape[1] // replicas
    vector_parts = vector_grads.reshape(2, chips, 1, part)

    def two_rows(values):
        pair = jnp.concatenate([v.astype(F32) for v in split(values)], 1)
        return jnp.pad(pair, ((0, 0), (0, owned - 2), (0, LANES - part)))

    def packed(side):
        block = lax.dynamic_index_in_dim(by_owner, side, 1, keepdims=False)
        return block, lax.dynamic_index_in_dim(vector_parts, side, 0, keepdims=False)

    block, vector = packed(1 - core)
    other = lax.ppermute(jnp.concatenate([block, two_rows(vector)], 2).astype(BF16), "c", SWAP).astype(F32)
    block, vector = packed(core)
    block = block + other[:, :, :cols]
    vector = vector + other[:, 0:1, cols : cols + part] + other[:, 1:2, cols : cols + part]
    arrived = exchange(jnp.concatenate([block, two_rows(vector)], 2).astype(BF16), CHIPS)

    shared_cols = 2 * cols + LANES
    shared = pl.pallas_call(
        share_kernel,
        out_shape=jax.ShapeDtypeStruct((chips, owned, shared_cols), BF16),
        in_specs=[VMEM] * 3,
        out_specs=VMEM,
        compiler_params=SMALL,
        name="share",
    )(arrived, momentum, master_owned)
    near = exchange(shared, CHIPS)
    far = lax.ppermute(near, "c", SWAP)
    left = pl.pallas_call(
        left_kernel,
        out_shape=jax.ShapeDtypeStruct((2 * tp, rank, half), BF16),
        in_specs=[VMEM] * 2,
        out_specs=VMEM,
        compiler_params=SMALL,
        name="left",
    )(near, warm_factor)
    left = exchange(left, ("c", "tp"))
    parts, vector = pl.pallas_call(
        power_kernel,
        out_shape=(
            jax.ShapeDtypeStruct((tp, rank, rows), BF16),
            jax.ShapeDtypeStruct((2, chips, LANES), F32),
        ),
        in_specs=[SMEM] + [VMEM] * 3,
        out_specs=(VMEM, VMEM),
        compiler_params=SMALL,
        name="power",
    )(place, left, near, far)
    parts = exchange(parts, "tp")
    inverse_one = pl.pallas_call(
        factor_kernel,
        out_shape=jax.ShapeDtypeStruct((rank, rank), F32),
        in_specs=[SMEM, VMEM, ANY],
        out_specs=VMEM,
        compiler_params=SMALL,
        name="factor",
    )(place, left, vector)
    vector_sum = vector[:, :, :part].reshape(-1)

    new_feedback, weight, new_momentum, new_master = pl.pallas_call(
        functools.partial(finish_kernel, replicas=replicas),
        out_shape=(
            jax.ShapeDtypeStruct(by_pair, F32),
            jax.ShapeDtypeStruct(by_pair, BF16),
            jax.ShapeDtypeStruct(momentum.shape, F32),
            jax.ShapeDtypeStruct(momentum.shape, F32),
        ),
        in_specs=[SMEM] + [VMEM] * 8,
        out_specs=(ANY, ANY, VMEM, VMEM),
        scratch_shapes=[
            pltpu.VMEM((3 * rank, rows), BF16),
            pltpu.VMEM((3 * rank, cols), BF16),
            pltpu.VMEM(by_pair, F32),
            pltpu.VMEM(by_pair, BF16),
            pltpu.VMEM((2, chips, owned, cols), BF16),
            pltpu.VMEM((2, chips, owned, cols), F32),
            pltpu.SemaphoreType.DMA((CHUNKS, 2)),
        ],
        compiler_params=LARGE,
        name="finish",
    )(
        place,
        parts,
        inverse_one,
        near,
        far,
        gradients.reshape(by_pair),
        feedback.reshape(by_pair),
        momentum,
        master_owned,
    )
    new_vector_momentum = MOMENTUM_RATE * vector_momentum + vector_sum / replicas
    new_vector_params = vector_params - LEARN_RATE * new_vector_momentum
    return (
        new_feedback.reshape(feedback.shape),
        new_momentum,
        new_master,
        weight.reshape(rows, cols),
        new_vector_params,
        new_vector_momentum,
    )


def solution(mesh):
    finer = Mesh(mesh.devices.reshape(8, 8, 2, mesh.shape["tp"]), ("y", "z", "c", "tp"))
    in_specs = (
        P(REP, None, "tp"),
        P(REP, None, "tp"),
        P("tp", None),
        P(REP, "tp"),
        P(REP, "tp"),
        P(REP, None),
        P(),
        P(),
    )
    out_specs = (P(REP, None, "tp"), P(REP, "tp"), P(REP, "tp"), P(None, "tp"), P(), P())
    return jax.shard_map(
        shards, mesh=finer, in_specs=in_specs, out_specs=out_specs, check_vma=False
    )
```

time: 116 us -> 99.4 us (0.86)
  blocking collectives: 23.5 us -> 50.6 us
  waiting for transfers between devices: 27.1 us -> 10.1 us
  other arithmetic: 19.3 us -> 3.35 us
  starting transfers between devices: 34.6 us -> 22.4 us
  Pallas kernels: 0 us -> 8.03 us
  matrix products: 6 us -> 0 us
    all_to_all x1 -> x2, blocking collectives: 23.5 us -> 50.6 us  [exchange(): return lax.all_to_all(array, axis, 0, 0, tiled=True)]
    all_to_all x3 -> x2, waiting for transfers between devices: 24.5 us -> 8.78 us  [exchange(): return lax.all_to_all(array, axis, 0, 0, tiled=True)]
    another operation x12 -> x2, other arithmetic: 13.5 us -> 0.18 us  [the longest x6 7.19 us: factor_of(): return jnp.linalg.cholesky(jnp.dot(left.T, left, precision=PRECISE))]
    all_to_all x3 -> x2, starting transfers between devices: 18.4 us -> 7.95 us  [exchange(): return lax.all_to_all(array, axis, 0, 0, tiled=True)]
    pallas_call x0 -> x5, Pallas kernels: none -> 8.03 us  [the longest x1 4.28 us: shards(): pl.pallas_call(functools.partial(finish_kernel, replicas=replicas), out_s...]
    dot_general x7 -> x0, matrix products: 5.35 us -> none  [the longest x1 2.24 us: shards(): approx = jnp.dot(ortho_two, right_two.T, precision=PRECISE) / replicas]
    ppermute x1, starting transfers between devices: 7.5 us -> 5.71 us  [shards(): far = lax.ppermute(near, 'c', SWAP)]
    ppermute x1, waiting for transfers between devices: 1.69 us -> 0.01 us  [shards(): far = lax.ppermute(near, 'c', SWAP)]
  transfers between devices with their start and end apart: 5 -> 4, of which waited for: 5 -> 3; matrix products, arithmetic and copies ran while one was open for 1% -> 2% of each run, Pallas kernels for 0% -> 3%
where the time goes in v2:
time: 99.4 us; the launch traced here: 98.1 us
  blocking collectives  50.6 us (51%)
  starting transfers between devices  22.4 us (23%)
  waiting for transfers between devices  10.1 us (10%)
  Pallas kernels  8.03 us (8%)
  other arithmetic  3.35 us (3%)
  local copies, waits for them, and re-layouts  2.84 us (3%)
    all_to_all x2, blocking collectives, exchange(): return lax.all_to_all(array, axis, 0, 0, tiled=True)  50.6 us
    all_to_all x2, waiting for transfers between devices, exchange(): return lax.all_to_all(array, axis, 0, 0, tiled=True)  8.78 us
    ppermute x1, starting transfers between devices, shards(): lax.ppermute(jnp.concatenate([block, two_rows(vector)], 2).astype(BF16),...  8.75 us
    all_to_all x2, starting transfers between devices, exchange(): return lax.all_to_all(array, axis, 0, 0, tiled=True)  7.95 us
    ppermute x1, starting transfers between devices, shards(): far = lax.ppermute(near, 'c', SWAP)  5.71 us
    pallas_call x1, Pallas kernels, shards(): pl.pallas_call(functools.partial(finish_kernel, replicas=replicas), out_s...  4.28 us
  transfers between devices with their start and end apart: 4, of which 3 were waited for; matrix products, arithmetic and copies ran while one was open for 2% of the time, Pallas kernels for 3%

profile of v2, /device:TPU:1, one launch (start us, length us, event | category | flops | bytes accessed | tf_op | source)
XLA Modules:
  0.0 98.1 jit_solution(5659149800206094701)
XLA Ops:
  0.6 0.7 copy-done.8
  1.4 0.1 reshape.75
  1.5 0.1 copy.33
  1.7 0.1 copy.34
  1.8 1.5 %convert_add_fusion = f32[1,1024,256]{2,1,0:T(8,128)S(1)} fusion(f32[1,1024,256]{2,1,0:T(8,128)} %param.9, bf16[1,1024,256]{2,1,0:T(8,128)(2,1)} %param.8), kind=kLoop, calls=%fused_computation | loop fusion | flops 524288 | bytes 2621440 | tf_op jit(solution)/shard_map/add | solution.py:211
  3.3 0.1 fusion.2
  3.4 8.7 %collective-permute-start = (bf16[64,8,384]{2,1,0:T(8,128)(2,1)S(1)}, bf16[64,8,384]{2,1,0:T(8,128)(2,1)S(1)}, u32[]{:S(2)}, u32[]{:S(2)}) collective-permute-start(bf16[64,8,384]{2,1,0:T(8,128)(2,1)S(1)} %fusion.2), channel_id=1, source_target_pairs={{0,4},{4,0},{1,5},{5,1},{2,6},{6,2},{3,7},{7,3},{8,12},{12,8},{9,1... | collective-permute-start | bytes 1179656 | tf_op jit(solution)/shard_map/ppermute | solution.py:225
  12.1 1.3 %collective-permute-done = bf16[64,8,384]{2,1,0:T(8,128)(2,1)S(1)} collective-permute-done((bf16[64,8,384]{2,1,0:T(8,128)(2,1)S(1)}, bf16[64,8,384]{2,1,0:T(8,128)(2,1)S(1)}, u32[]{:S(2)}, u32[]{:S(2)}) %collective-permute-start) | collective-permute-done | bytes 393248 | tf_op jit(solution)/shard_map/ppermute | solution.py:225
  13.4 0.1 convert_element_type.79
  13.5 0.1 fusion.1
  13.6 0.1 fusion.11
  13.7 0.1 fusion.9
  13.9 0.0 copy-start.4
  13.9 25.7 %all_to_all.20.arrived = bf16[64,8,384]{2,1,0:T(8,128)(2,1)S(1)} all-to-all(bf16[64,8,384]{2,1,0:T(8,128)(2,1)S(1)} %pad_maximum_fusion), channel_id=1, replica_groups=mesh['y'=8,'z'=8,'c'=2,'tp'=4] {'y','z'}, dimensions={0} | all-to-all | bytes 786432 | tf_op jit(solution)/shard_map/all_to_all | solution.py:35
  39.7 0.1 share.1
  39.8 24.8 %all_to_all.21.near = bf16[64,8,640]{2,1,0:T(8,128)(2,1)S(1)} all-to-all(bf16[64,8,640]{2,1,0:T(8,128)(2,1)S(1)} %share.1), channel_id=1, replica_groups=mesh['y'=8,'z'=8,'c'=2,'tp'=4] {'y','z'}, dimensions={0} | all-to-all | bytes 1310720 | tf_op jit(solution)/shard_map/all_to_all | solution.py:35
  64.6 5.7 %collective-permute-start.1 = (bf16[64,8,640]{2,1,0:T(8,128)(2,1)S(1)}, bf16[64,8,640]{2,1,0:T(8,128)(2,1)S(1)}, u32[]{:S(2)}, u32[]{:S(2)}) collective-permute-start(bf16[64,8,640]{2,1,0:T(8,128)(2,1)S(1)} %all_to_all.21.near), channel_id=1, source_target_pairs={{0,4},{4,0},{1,5},{5,1},{2,6},{6,2},{3,7},{7,3},{8,12},{12,8},{9,1... | collective-permute-start | bytes 1966088 | tf_op jit(solution)/shard_map/ppermute | solution.py:241
  70.3 0.1 copy.35.factor
  70.4 0.9 left.1
  71.3 4.4 %all-to-all-start.2 = ((bf16[8,32,512]{2,1,0:T(8,128)(2,1)}), bf16[8,32,512]{2,1,0:T(8,128)(2,1)S(1)}, u32[]{:S(2)}, u32[]{:S(2)}) async-start(bf16[8,32,512]{2,1,0:T(8,128)(2,1)} %left.1), calls=%async_computation.2 | async-start | bytes 524288 | tf_op jit(solution)/shard_map/all_to_all | solution.py:35
  75.8 0.1 pad_add_fusion.place
  75.8 6.5 %all-to-all-done.2.arrived = bf16[8,32,512]{2,1,0:T(8,128)(2,1)S(1)} async-done(((bf16[8,32,512]{2,1,0:T(8,128)(2,1)}), bf16[8,32,512]{2,1,0:T(8,128)(2,1)S(1)}, u32[]{:S(2)}, u32[]{:S(2)}) %all-to-all-start.2) | async-done | bytes 262176 | tf_op jit(solution)/shard_map/all_to_all | solution.py:35
  82.3 1.2 %power.1 = (bf16[4,32,1024]{2,1,0:T(8,128)(2,1)S(1)}, f32[2,64,128]{2,1,0:T(8,128)S(1)}) custom-call(s32[2]{0:T(128)S(1)} %pad_add_fusion.place, bf16[8,32,512]{2,1,0:T(8,128)(2,1)S(1)} %all-to-all-done.2.arrived, bf16[64,8,640]{2,1,0:T(8,128)(2,1)S(1)} %all_to_all.21.near, bf16[64,8,640]{2,1,0:T(8,128)(2,1)S(1)} %collective-permute-done.1.far), custom_call_target="tpu_custom_call" | custom-call | tf_op jit(solution)/shard_map/power/pallas_call | solution.py:251
  83.5 0.0 copy-start.2
  83.5 0.7 copy-done.2
  84.2 3.5 %all-to-all-start.3 = ((bf16[4,32,1024]{2,1,0:T(8,128)(2,1)}), bf16[4,32,1024]{2,1,0:T(8,128)(2,1)S(1)}, u32[]{:S(2)}, u32[]{:S(2)}) async-start(bf16[4,32,1024]{2,1,0:T(8,128)(2,1)} %copy-done.2), calls=%async_computation.3 | async-start | bytes 524288 | tf_op jit(solution)/shard_map/all_to_all | solution.py:35
  87.7 0.6 slice_multiply_fusion
  88.4 0.9 div.10
  89.3 1.5 %factor.2.inverse_one = f32[32,32]{1,0:T(8,128)S(1)} custom-call(s32[2]{0:T(128)S(1)} %pad_add_fusion.place, bf16[8,32,512]{2,1,0:T(8,128)(2,1)S(1)} %all-to-all-done.2.arrived, f32[2,64,128]{2,1,0:T(8,128)S(1)} %get-tuple-element.13.after), custom_call_target="tpu_custom_call" | custom-call | tf_op jit(solution)/shard_map/factor/pallas_call | solution.py:263
  90.9 0.6 multiply_subtract_fusion
  91.5 2.3 %all-to-all-done.3.parts = bf16[4,32,1024]{2,1,0:T(8,128)(2,1)S(1)} async-done(((bf16[4,32,1024]{2,1,0:T(8,128)(2,1)}), bf16[4,32,1024]{2,1,0:T(8,128)(2,1)S(1)}, u32[]{:S(2)}, u32[]{:S(2)}) %all-to-all-start.3) | async-done | bytes 262176 | tf_op jit(solution)/shard_map/all_to_all | solution.py:35
  93.8 4.3 %finish.1 = (f32[64,16,256]{2,1,0:T(8,128)}, bf16[64,16,256]{2,1,0:T(8,128)(2,1)}, f32[8,256]{1,0:T(8,128)}, f32[8,256]{1,0:T(8,128)}) custom-call(s32[2]{0:T(128)S(1)} %pad_add_fusion.place, bf16[4,32,1024]{2,1,0:T(8,128)(2,1)S(1)} %all-to-all-done.3.parts, f32[32,32]{1,0:T(8,128)S(1)} %factor.2.inverse_one, bf16[64,8,640]{2,1,0:T(8,128)(2,1)S(1)} %all_to_all.21.near, ...), custom_call_target="tpu_custom_call" | custom-call | tf_op jit(solution)/shard_map/finish/pallas_call | solution.py:273
  (23 shorter events, 0.3 us)
Async XLA Ops:
  0.6 0.7 copy-start.8
  3.4 10.1 %collective-permute-start = (bf16[64,8,384]{2,1,0:T(8,128)(2,1)S(1)}, bf16[64,8,384]{2,1,0:T(8,128)(2,1)S(1)}, u32[]{:S(2)}, u32[]{:S(2)}) collective-permute-start(bf16[64,8,384]{2,1,0:T(8,128)(2,1)S(1)} %fusion.2), channel_id=1, source_target_pairs={{0,4},{4,0},{1,5},{5,1},{2,6},{6,2},{3,7},{7,3},{8,12},{12,8},{9,1... | collective-permute-start | bytes 1179656 | tf_op jit(solution)/shard_map/ppermute | solution.py:225
  13.9 25.8 %copy-start.3 = (f32[8,256]{1,0:T(8,128)S(1)}, f32[8,256]{1,0:T(8,128)}, u32[]{:S(2)}) copy-start(f32[8,256]{1,0:T(8,128)} %momentum.3) | copy-start | bytes 24580
  13.9 25.8 %copy-start.4 = (f32[8,256]{1,0:T(8,128)S(1)}, f32[8,256]{1,0:T(8,128)}, u32[]{:S(2)}) copy-start(f32[8,256]{1,0:T(8,128)} %master.3) | copy-start | bytes 24580
  39.8 30.5 %copy-start.5 = (f32[256,32]{0,1:T(8,128)S(1)}, f32[256,32]{0,1:T(8,128)}, u32[]{:S(2)}) copy-start(f32[256,32]{0,1:T(8,128)} %param.10) | copy-start | bytes 98308
  64.6 17.7 %collective-permute-start.1 = (bf16[64,8,640]{2,1,0:T(8,128)(2,1)S(1)}, bf16[64,8,640]{2,1,0:T(8,128)(2,1)S(1)}, u32[]{:S(2)}, u32[]{:S(2)}) collective-permute-start(bf16[64,8,640]{2,1,0:T(8,128)(2,1)S(1)} %all_to_all.21.near), channel_id=1, source_target_pairs={{0,4},{4,0},{1,5},{5,1},{2,6},{6,2},{3,7},{7,3},{8,12},{12,8},{9,1... | collective-permute-start | bytes 1966088 | tf_op jit(solution)/shard_map/ppermute | solution.py:241
  71.3 10.9 %all-to-all-start.2 = ((bf16[8,32,512]{2,1,0:T(8,128)(2,1)}), bf16[8,32,512]{2,1,0:T(8,128)(2,1)S(1)}, u32[]{:S(2)}, u32[]{:S(2)}) async-start(bf16[8,32,512]{2,1,0:T(8,128)(2,1)} %left.1), calls=%async_computation.2 | async-start | bytes 524288 | tf_op jit(solution)/shard_map/all_to_all | solution.py:35
  75.8 18.0 %copy-start = (f32[1,1024,256]{2,1,0:T(8,128)S(1)}, f32[1,1024,256]{2,1,0:T(8,128)}, u32[]{:S(2)}) copy-start(f32[1,1024,256]{2,1,0:T(8,128)} %param.9) | copy-start | bytes 3145732
  83.5 0.7 copy-start.2
  84.2 9.7 %copy-start.1 = (bf16[1,1024,256]{2,1,0:T(8,128)(2,1)S(1)}, bf16[1,1024,256]{2,1,0:T(8,128)(2,1)}, u32[]{:S(2)}) copy-start(bf16[1,1024,256]{2,1,0:T(8,128)(2,1)} %param.8) | copy-start | bytes 1572868
  84.2 9.6 %all-to-all-start.3 = ((bf16[4,32,1024]{2,1,0:T(8,128)(2,1)}), bf16[4,32,1024]{2,1,0:T(8,128)(2,1)S(1)}, u32[]{:S(2)}, u32[]{:S(2)}) async-start(bf16[4,32,1024]{2,1,0:T(8,128)(2,1)} %copy-done.2), calls=%async_computation.3 | async-start | bytes 524288 | tf_op jit(solution)/shard_map/all_to_all | solution.py:35
  89.3 1.6 %copy-start.6 = (f32[2560]{0:T(1024)S(1)}, f32[2560]{0:T(1024)}, u32[]{:S(2)}) copy-start(f32[2560]{0:T(1024)} %param.14) | copy-start | bytes 30724
  89.3 1.6 %copy-start.7 = (f32[2560]{0:T(1024)S(1)}, f32[2560]{0:T(1024)}, u32[]{:S(2)}) copy-start(f32[2560]{0:T(1024)} %param.15) | copy-start | bytes 30724

commit v3 on v2

--- a/solution.py
+++ b/solution.py
@@ -19,6 +19,7 @@
 LANES = 128
 PIVOTS = 8
 CHUNKS = 4
+TP = 4
 VMEM = pl.BlockSpec(memory_space=pltpu.VMEM)
 SMEM = pl.BlockSpec(memory_space=pltpu.SMEM)
 ANY = pl.BlockSpec(memory_space=pl.ANY)
@@ -72,14 +73,60 @@
     return lower_inverse(product(left, left, ((1,), (1,)), PRECISE))
 
 
-def share_kernel(arrived, momentum, master, out):
-    cols = momentum.shape[1]
+def quarter_of(place, vector):
+    count = vector.shape[0] // TP
+    rows = [vector[place[2] * count + j] for j in range(count)]
+    return jnp.concatenate(rows + [jnp.zeros((8 - count, LANES), F32)], 0)
+
+
+def half_of(side, gradients, feedback, narrow, wide, sems, store):
+    step = gradients.shape[0] // CHUNKS
+    spans = [slice(chunk * step, (chunk + 1) * step) for chunk in range(CHUNKS)]
+    copies = []
+    for chunk, span in enumerate(spans):
+        for which, (source, target) in enumerate(((gradients, narrow), (feedback, wide))):
+            copy = pltpu.make_async_copy(source.at[span, side], target.at[span], sems.at[chunk, which])
+            copy.start()
+            copies.append(copy)
+    for chunk, span in enumerate(spans):
+        copies[2 * chunk].wait()
+        copies[2 * chunk + 1].wait()
+        store(span, narrow[span].astype(F32) + wide[span])
+
+
+def send_kernel(place, gradients, feedback, vector, out, narrow, wide, sems):
+    def store(span, values):
+        out[span] = values.astype(BF16)
+
+    out[gradients.shape[0]] = jnp.concatenate(split(quarter_of(place, vector)), 1)
+    half_of(1 - place[0], gradients, feedback, narrow, wide, sems, store)
+
+
+def keep_kernel(place, gradients, feedback, after, out, narrow, wide, sems):
+    del after
+
+    def store(span, values):
+        out[span] = values
+
+    half_of(place[0], gradients, feedback, narrow, wide, sems, store)
+
+
+def pair_kernel(kept, received, out):
+    out[...] = (kept[...] + received[: kept.shape[0]].astype(F32)).astype(BF16)
+
+
+def packed_rows(rows):
+    high, low = split(rows)
+    return jnp.concatenate([high.astype(F32), low.astype(F32), jnp.zeros((2, LANES), F32)], 0)
+
+
+def share_kernel(place, arrived, received, vector, momentum, master, out):
     total = jnp.sum(arrived[...].astype(F32), axis=0)
-    high, low = split(total[0:1, cols:] + total[1:2, cols:])
-    row = lax.broadcasted_iota(jnp.int32, (total.shape[0], LANES), 0)
-    vector = jnp.where(row == 0, high.astype(F32), jnp.where(row == 1, low.astype(F32), 0.0))
+    other = received[received.shape[0] - 1].astype(F32)
+    quarter = quarter_of(place, vector) + other[:, :LANES] + other[:, LANES:]
+    rows = jnp.where(place[0] == 0, quarter[0:3], quarter[3:6])
     base = master[...] - LEARN_RATE * MOMENTUM_RATE * momentum[...]
-    shared = jnp.concatenate([total[:, :cols], vector, base], 1).astype(BF16)
+    shared = jnp.concatenate([total, packed_rows(rows), base], 1).astype(BF16)
     out[...] = jnp.broadcast_to(shared, out.shape)
 
 
@@ -88,26 +135,28 @@
 
 
 def left_kernel(near, factor, out):
-    cols = factor.shape[0]
+    cols, _ = factor.shape
     left = times_exact(factor[...].T, matrix_of(near, cols), ((1,), (1,)))
-    out[...] = jnp.broadcast_to(left.astype(BF16), out.shape)
+    spread = jnp.sum(near[:, :, cols : cols + LANES].astype(F32), axis=0)
+    rows = packed_rows(spread[0:3] + spread[3:6])
+    rows = jnp.concatenate([rows, jnp.zeros((8, left.shape[1] - LANES), F32)], 1)
+    both = jnp.concatenate([left, rows], 0).astype(BF16)
+    out[...] = jnp.broadcast_to(both, out.shape)
 
 
 def left_sum(place, arrived):
     tp = arrived.shape[0] // 2
+    rank = arrived.shape[1] - 8
     core = place[0]
 
     def half(side):
-        return jnp.sum(arrived[pl.ds(side * tp, tp)].astype(F32), axis=0)
+        return jnp.sum(arrived[pl.ds(side * tp, tp), :rank].astype(F32), axis=0)
 
     return half(core), half(1 - core)
 
 
-def power_kernel(place, arrived, near, far, out, vector):
+def power_kernel(place, arrived, near, far, out):
     cols = near.shape[2] * 2 // 5
-    core = place[0]
-    for side, ref in ((core, near), (1 - core, far)):
-        vector[side] = ref[:, 0, cols : cols + LANES].astype(F32) + ref[:, 1, cols : cols + LANES].astype(F32)
     own, other = left_sum(place, arrived)
     near_matrix, far_matrix = matrix_of(near, cols), matrix_of(far, cols)
     right = times_exact(own, near_matrix, ((1,), (0,))) + times_exact(other, far_matrix, ((1,), (0,)))
@@ -117,8 +166,16 @@
         out[:, :, side * half : (side + 1) * half] = jnp.broadcast_to(left, (out.shape[0], *left.shape))
 
 
-def factor_kernel(place, arrived, after, out):
+def factor_kernel(place, arrived, after, out, vector):
     del after
+    peers, filled = arrived.shape[:2]
+    tp, rank = peers // 2, filled - 8
+    count = vector.shape[0] // tp
+    for peer in range(peers):
+        side, column = peer // tp, peer % tp
+        tile = arrived[peer, rank:, :LANES].astype(F32)
+        for row in range(3 if side == 0 else count - 3):
+            vector[column * count + 3 * side + row] = tile[row : row + 1] + tile[row + 3 : row + 4]
     own, other = left_sum(place, arrived)
     out[...] = gram_inverse(jnp.concatenate([own, other], 1))
 
@@ -205,70 +262,82 @@
     owned = momentum.shape[0]
     rank = warm_factor.shape[1]
     half = rows // 2
-    place = jnp.stack([core, lax.axis_index(CHIPS)]).astype(jnp.int32)
+    place = jnp.stack([core, lax.axis_index(CHIPS), lax.axis_index("tp")]).astype(jnp.int32)
     by_pair = (chips, 2 * owned, cols)
-
-    combined = gradients[0].astype(F32) + feedback[0]
-    by_owner = combined.reshape(chips, 2, owned, cols)
-    part = vector_grads.shape[1] // replicas
-    vector_parts = vector_grads.reshape(2, chips, 1, part)
-
-    def two_rows(values):
-        pair = jnp.concatenate([v.astype(F32) for v in split(values)], 1)
-        return jnp.pad(pair, ((0, 0), (0, owned - 2), (0, LANES - part)))
-
-    def packed(side):
-        block = lax.dynamic_index_in_dim(by_owner, side, 1, keepdims=False)
-        return block, lax.dynamic_index_in_dim(vector_parts, side, 0, keepdims=False)
-
-    block, vector = packed(1 - core)
-    other = lax.ppermute(jnp.concatenate([block, two_rows(vector)], 2).astype(BF16), "c", SWAP).astype(F32)
-    block, vector = packed(core)
-    block = block + other[:, :, :cols]
-    vector = vector + other[:, 0:1, cols : cols + part] + other[:, 1:2, cols : cols + part]
-    arrived = exchange(jnp.concatenate([block, two_rows(vector)], 2).astype(BF16), CHIPS)
+    by_owner = (chips, 2, owned, cols)
+    lines = vector_grads.reshape(-1, 1, LANES)
+    halves = (gradients.reshape(by_owner), feedback.reshape(by_owner))
+    buffers = [
+        pltpu.VMEM((chips, owned, cols), BF16),
+        pltpu.VMEM((chips, owned, cols), F32),
+        pltpu.SemaphoreType.DMA((CHUNKS, 2)),
+    ]
+
+    sent = pl.pallas_call(
+        send_kernel,
+        out_shape=jax.ShapeDtypeStruct((chips + 1, owned, cols), BF16),
+        in_specs=[SMEM, ANY, ANY, VMEM],
+        out_specs=VMEM,
+        scratch_shapes=buffers,
+        name="send",
+    )(place, *halves, lines)
+    received = lax.ppermute(sent, "c", SWAP)
+    kept = pl.pallas_call(
+        keep_kernel,
+        out_shape=jax.ShapeDtypeStruct((chips, owned, cols), F32),
+        in_specs=[SMEM, ANY, ANY, ANY],
+        out_specs=VMEM,
+        scratch_shapes=buffers,
+        name="keep",
+    )(place, *halves, sent)
+    paired = pl.pallas_call(
+        pair_kernel,
+        out_shape=jax.ShapeDtypeStruct((chips, owned, cols), BF16),
+        in_specs=[VMEM] * 2,
+        out_specs=VMEM,
+        compiler_params=SMALL,
+        name="pair",
+    )(kept, received)
+    arrived = exchange(paired, CHIPS)
 
     shared_cols = 2 * cols + LANES
     shared = pl.pallas_call(
         share_kernel,
         out_shape=jax.ShapeDtypeStruct((chips, owned, shared_cols), BF16),
-        in_specs=[VMEM] * 3,
+        in_specs=[SMEM] + [VMEM] * 5,
         out_specs=VMEM,
         compiler_params=SMALL,
         name="share",
-    )(arrived, momentum, master_owned)
+    )(place, arrived, received, lines, momentum, master_owned)
     near = exchange(shared, CHIPS)
     far = lax.ppermute(near, "c", SWAP)
     left = pl.pallas_call(
         left_kernel,
-        out_shape=jax.ShapeDtypeStruct((2 * tp, rank, half), BF16),
+        out_shape=jax.ShapeDtypeStruct((2 * tp, rank + 8, half), BF16),
         in_specs=[VMEM] * 2,
         out_specs=VMEM,
         compiler_params=SMALL,
         name="left",
     )(near, warm_factor)
     left = exchange(left, ("c", "tp"))
-    parts, vector = pl.pallas_call(
+    parts = pl.pallas_call(
         power_kernel,
-        out_shape=(
-            jax.ShapeDtypeStruct((tp, rank, rows), BF16),
-            jax.ShapeDtypeStruct((2, chips, LANES), F32),
-        ),
+        out_shape=jax.ShapeDtypeStruct((tp, rank, rows), BF16),
         in_specs=[SMEM] + [VMEM] * 3,
-        out_specs=(VMEM, VMEM),
+        out_specs=VMEM,
         compiler_params=SMALL,
         name="power",
     )(place, left, near, far)
-    parts = exchange(parts, "tp")
-    inverse_one = pl.pallas_call(
+    inverse_one, vector = pl.pallas_call(
         factor_kernel,
-        out_shape=jax.ShapeDtypeStruct((rank, rank), F32),
+        out_shape=(jax.ShapeDtypeStruct((rank, rank), F32), jax.ShapeDtypeStruct(lines.shape, F32)),
         in_specs=[SMEM, VMEM, ANY],
-        out_specs=VMEM,
+        out_specs=(VMEM, VMEM),
         compiler_params=SMALL,
         name="factor",
-    )(place, left, vector)
-    vector_sum = vector[:, :, :part].reshape(-1)
+    )(place, left, parts)
+    parts = exchange(parts, "tp")
+    vector_sum = vector.reshape(-1)
 
     new_feedback, weight, new_momentum, new_master = pl.pallas_call(
         functools.partial(finish_kernel, replicas=replicas),

time: 99.4 us -> 100 us (level)
  blocking collectives: 50.6 us -> 59.7 us
  waiting for transfers between devices: 10.1 us -> 3.17 us
  Pallas kernels: 8.03 us -> 14 us
  starting transfers between devices: 22.4 us -> 18 us
  other arithmetic: 3.35 us -> 1.23 us
    all_to_all x2 -> x3, blocking collectives: 50.6 us -> 59.7 us  [exchange(): return lax.all_to_all(array, axis, 0, 0, tiled=True)]
    all_to_all x2 -> x1, waiting for transfers between devices: 8.78 us -> 3.16 us  [exchange(): return lax.all_to_all(array, axis, 0, 0, tiled=True)]
    pallas_call x3 -> x6, Pallas kernels: 3.64 us -> 9.1 us  [the longest x1 2.76 us: shards(): pl.pallas_call(keep_kernel, out_shape=jax.ShapeDtypeStruct((chips, owned,...]
    all_to_all x2 -> x1, starting transfers between devices: 7.95 us -> 3.54 us  [exchange(): return lax.all_to_all(array, axis, 0, 0, tiled=True)]
    add x1 -> x0, other arithmetic: 1.46 us -> none  [shards(): combined = gradients[0].astype(F32) + feedback[0]]
    ppermute x1, waiting for transfers between devices: 1.33 us -> 0.01 us  [shards(): received = lax.ppermute(sent, 'c', SWAP)]
  transfers between devices with their start and end apart: 4 -> 3, of which waited for: 3 -> 1; matrix products, arithmetic and copies ran while one was open for 2% -> 1% of each run, Pallas kernels for 3% -> 5%
where the time goes in v3:
time: 100 us; the launch traced here: 98.8 us
  blocking collectives  59.7 us (60%)
  starting transfers between devices  18 us (18%)
  Pallas kernels  14 us (14%)
  waiting for transfers between devices  3.17 us (3%)
  local copies, waits for them, and re-layouts  1.84 us (2%)
  other arithmetic  1.23 us (1%)
    all_to_all x3, blocking collectives, exchange(): return lax.all_to_all(array, axis, 0, 0, tiled=True)  59.7 us
    ppermute x1, starting transfers between devices, shards(): received = lax.ppermute(sent, 'c', SWAP)  8.75 us
    ppermute x1, starting transfers between devices, shards(): far = lax.ppermute(near, 'c', SWAP)  5.68 us
    pallas_call x1, Pallas kernels, shards(): pl.pallas_call(functools.partial(finish_kernel, replicas=replicas), out_s...  4.28 us
    all_to_all x1, starting transfers between devices, exchange(): return lax.all_to_all(array, axis, 0, 0, tiled=True)  3.54 us
    all_to_all x1, waiting for transfers between devices, exchange(): return lax.all_to_all(array, axis, 0, 0, tiled=True)  3.16 us
    pallas_call x1, Pallas kernels, shards(): pl.pallas_call(keep_kernel, out_shape=jax.ShapeDtypeStruct((chips, owned,...  2.76 us
    pallas_call x1, Pallas kernels, shards(): pl.pallas_call(send_kernel, out_shape=jax.ShapeDtypeStruct((chips + 1, ow...  2.71 us
  transfers between devices with their start and end apart: 3, of which 1 were waited for; matrix products, arithmetic and copies ran while one was open for 1% of the time, Pallas kernels for 5%

profile of v3, /device:TPU:1, one launch (start us, length us, event | category | flops | bytes accessed | tf_op | source)
XLA Modules:
  0.0 98.8 jit_solution(9839908732288927415)
XLA Ops:
  0.6 0.6 pad_add_fusion.place
  1.2 2.7 %send.1.after = bf16[65,8,256]{2,1,0:T(8,128)(2,1)} custom-call(s32[3]{0:T(128)} %pad_add_fusion.place, bf16[64,2,8,256]{3,2,1,0:T(8,128)(2,1)} %bitcast.16, f32[64,2,8,256]{3,2,1,0:T(8,128)} %bitcast.13, f32[20,1,128]{2,1,0:T(1,128)} %bitcast.19), custom_call_target="tpu_custom_call" | custom-call | tf_op jit(solution)/shard_map/send/pallas_call | solution.py:276
  3.9 8.7 %collective-permute-start = (bf16[65,8,256]{2,1,0:T(8,128)(2,1)}, bf16[65,8,256]{2,1,0:T(8,128)(2,1)S(1)}, u32[]{:S(2)}, u32[]{:S(2)}) collective-permute-start(bf16[65,8,256]{2,1,0:T(8,128)(2,1)} %send.1.after), channel_id=1, source_target_pairs={{0,4},{4,0},{1,5},{5,1},{2,6},{6,2},{3,7},{7,3},{8,12},{12,8},{9,1... | collective-permute-start | bytes 798728 | tf_op jit(solution)/shard_map/ppermute | solution.py:284
  12.7 2.8 %keep.1.kept = f32[64,8,256]{2,1,0:T(8,128)} custom-call(s32[3]{0:T(128)} %pad_add_fusion.place, bf16[64,2,8,256]{3,2,1,0:T(8,128)(2,1)} %bitcast.17, f32[64,2,8,256]{3,2,1,0:T(8,128)} %bitcast.14, bf16[65,8,256]{2,1,0:T(8,128)(2,1)} %send.1.after), custom_call_target="tpu_custom_call" | custom-call | tf_op jit(solution)/shard_map/keep/pallas_call | solution.py:285
  15.5 0.0 collective-permute-done.received
  15.5 0.0 copy-start.2
  15.5 1.0 %copy-done.2 = f32[64,8,256]{2,1,0:T(8,128)S(1)} copy-done((f32[64,8,256]{2,1,0:T(8,128)S(1)}, f32[64,8,256]{2,1,0:T(8,128)}, u32[]{:S(2)}) %copy-start.2) | copy-done | bytes 524312
  16.5 0.1 pair.1
  16.6 0.0 copy-start.3
  16.6 0.0 copy-start.4
  16.6 0.0 copy-start.5
  16.6 0.0 copy-start.6
  16.6 24.4 %all_to_all.20.arrived = bf16[64,8,256]{2,1,0:T(8,128)(2,1)S(1)} all-to-all(bf16[64,8,256]{2,1,0:T(8,128)(2,1)S(1)} %pair.1), channel_id=1, replica_groups=mesh['y'=8,'z'=8,'c'=2,'tp'=4] {'y','z'}, dimensions={0} | all-to-all | bytes 524288 | tf_op jit(solution)/shard_map/all_to_all | solution.py:36
  41.0 0.0 copy-done.3
  41.0 0.0 copy-done.4
  41.0 0.0 copy-done.6
  41.0 0.6 share.1
  41.7 0.0 copy-start.7
  41.7 23.6 %all_to_all.21.near = bf16[64,8,640]{2,1,0:T(8,128)(2,1)S(1)} all-to-all(bf16[64,8,640]{2,1,0:T(8,128)(2,1)S(1)} %share.1), channel_id=1, replica_groups=mesh['y'=8,'z'=8,'c'=2,'tp'=4] {'y','z'}, dimensions={0} | all-to-all | bytes 1310720 | tf_op jit(solution)/shard_map/all_to_all | solution.py:36
  65.3 5.7 %collective-permute-start.1 = (bf16[64,8,640]{2,1,0:T(8,128)(2,1)S(1)}, bf16[64,8,640]{2,1,0:T(8,128)(2,1)S(1)}, u32[]{:S(2)}, u32[]{:S(2)}) collective-permute-start(bf16[64,8,640]{2,1,0:T(8,128)(2,1)S(1)} %all_to_all.21.near), channel_id=1, source_target_pairs={{0,4},{4,0},{1,5},{5,1},{2,6},{6,2},{3,7},{7,3},{8,12},{12,8},{9,1... | collective-permute-start | bytes 1966088 | tf_op jit(solution)/shard_map/ppermute | solution.py:313
  71.0 0.1 copy.14.factor
  71.1 0.2 left.1
  71.3 11.8 %all_to_all.22.arrived = bf16[8,40,512]{2,1,0:T(8,128)(2,1)S(1)} all-to-all(bf16[8,40,512]{2,1,0:T(8,128)(2,1)S(1)} %left.1), channel_id=1, replica_groups=mesh['y'=8,'z'=8,'c'=2,'tp'=4] {'c','tp'}, dimensions={0} | all-to-all | bytes 655360 | tf_op jit(solution)/shard_map/all_to_all | solution.py:36
  83.1 0.0 collective-permute-done.1.far
  83.1 1.8 %power.1.after = bf16[4,32,1024]{2,1,0:T(8,128)(2,1)} custom-call(s32[3]{0:T(128)S(1)} %copy-done.6, bf16[8,40,512]{2,1,0:T(8,128)(2,1)S(1)} %all_to_all.22.arrived, bf16[64,8,640]{2,1,0:T(8,128)(2,1)S(1)} %all_to_all.21.near, bf16[64,8,640]{2,1,0:T(8,128)(2,1)S(1)} %collective-permute-done.1.far), custom_call_target="tpu_custom_call" | custom-call | tf_op jit(solution)/shard_map/power/pallas_call | solution.py:323
  84.9 3.5 %all-to-all-start.3 = ((bf16[4,32,1024]{2,1,0:T(8,128)(2,1)}), bf16[4,32,1024]{2,1,0:T(8,128)(2,1)S(1)}, u32[]{:S(2)}, u32[]{:S(2)}) async-start(bf16[4,32,1024]{2,1,0:T(8,128)(2,1)} %power.1.after), calls=%async_computation.3 | async-start | bytes 524288 | tf_op jit(solution)/shard_map/all_to_all | solution.py:36
  88.4 0.0 copy-start.9
  88.4 1.5 %factor.2 = (f32[32,32]{1,0:T(8,128)S(1)}, f32[20,1,128]{2,1,0:T(1,128)S(1)}) custom-call(s32[3]{0:T(128)S(1)} %copy-done.6, bf16[8,40,512]{2,1,0:T(8,128)(2,1)S(1)} %all_to_all.22.arrived, bf16[4,32,1024]{2,1,0:T(8,128)(2,1)} %power.1.after), custom_call_target="tpu_custom_call" | custom-call | tf_op jit(solution)/shard_map/factor/pallas_call | solution.py:331
  90.0 0.7 copy-done.8
  90.7 0.6 multiply_subtract_fusion
  91.3 3.2 %all-to-all-done.3.parts = bf16[4,32,1024]{2,1,0:T(8,128)(2,1)S(1)} async-done(((bf16[4,32,1024]{2,1,0:T(8,128)(2,1)}), bf16[4,32,1024]{2,1,0:T(8,128)(2,1)S(1)}, u32[]{:S(2)}, u32[]{:S(2)}) %all-to-all-start.3) | async-done | bytes 262176 | tf_op jit(solution)/shard_map/all_to_all | solution.py:36
  94.5 4.3 %finish.1 = (f32[64,16,256]{2,1,0:T(8,128)}, bf16[64,16,256]{2,1,0:T(8,128)(2,1)}, f32[8,256]{1,0:T(8,128)}, f32[8,256]{1,0:T(8,128)}) custom-call(s32[3]{0:T(128)S(1)} %copy-done.6, bf16[4,32,1024]{2,1,0:T(8,128)(2,1)S(1)} %all-to-all-done.3.parts, f32[32,32]{1,0:T(8,128)S(1)} %get-tuple-element.12.inverse_one, bf16[64,8,640]{2,1,0:T(8,128)(2,1)S(1)} %all_to_all.21.near, ...), custom_call_target="tpu_custom_call" | custom-call | tf_op jit(solution)/shard_map/finish/pallas_call | solution.py:342
  (9 shorter events, 0.1 us)
Async XLA Ops:
  3.9 11.5 %collective-permute-start = (bf16[65,8,256]{2,1,0:T(8,128)(2,1)}, bf16[65,8,256]{2,1,0:T(8,128)(2,1)S(1)}, u32[]{:S(2)}, u32[]{:S(2)}) collective-permute-start(bf16[65,8,256]{2,1,0:T(8,128)(2,1)} %send.1.after), channel_id=1, source_target_pairs={{0,4},{4,0},{1,5},{5,1},{2,6},{6,2},{3,7},{7,3},{8,12},{12,8},{9,1... | collective-permute-start | bytes 798728 | tf_op jit(solution)/shard_map/ppermute | solution.py:284
  15.5 1.0 %copy-start.2 = (f32[64,8,256]{2,1,0:T(8,128)S(1)}, f32[64,8,256]{2,1,0:T(8,128)}, u32[]{:S(2)}) copy-start(f32[64,8,256]{2,1,0:T(8,128)} %keep.1.kept) | copy-start | bytes 1572868
  16.6 24.4 %copy-start.3 = (f32[1,2560]{1,0:T(1,128)S(1)}, f32[1,2560]{1,0:T(1,128)}, u32[]{:S(2)}) copy-start(f32[1,2560]{1,0:T(1,128)} %param.13) | copy-start | bytes 30724
  16.6 24.4 %copy-start.4 = (f32[8,256]{1,0:T(8,128)S(1)}, f32[8,256]{1,0:T(8,128)}, u32[]{:S(2)}) copy-start(f32[8,256]{1,0:T(8,128)} %momentum.3) | copy-start | bytes 24580
  16.6 24.4 %copy-start.5 = (f32[8,256]{1,0:T(8,128)S(1)}, f32[8,256]{1,0:T(8,128)}, u32[]{:S(2)}) copy-start(f32[8,256]{1,0:T(8,128)} %master.3) | copy-start | bytes 24580
  16.6 24.4 %copy-start.6 = (s32[3]{0:T(128)S(1)}, s32[3]{0:T(128)}, u32[]{:S(2)}) copy-start(s32[3]{0:T(128)} %pad_add_fusion.place) | copy-start | bytes 40
  41.7 29.3 %copy-start.7 = (f32[256,32]{0,1:T(8,128)S(1)}, f32[256,32]{0,1:T(8,128)}, u32[]{:S(2)}) copy-start(f32[256,32]{0,1:T(8,128)} %param.10) | copy-start | bytes 98308
  65.3 17.8 %collective-permute-start.1 = (bf16[64,8,640]{2,1,0:T(8,128)(2,1)S(1)}, bf16[64,8,640]{2,1,0:T(8,128)(2,1)S(1)}, u32[]{:S(2)}, u32[]{:S(2)}) collective-permute-start(bf16[64,8,640]{2,1,0:T(8,128)(2,1)S(1)} %all_to_all.21.near), channel_id=1, source_target_pairs={{0,4},{4,0},{1,5},{5,1},{2,6},{6,2},{3,7},{7,3},{8,12},{12,8},{9,1... | collective-permute-start | bytes 1966088 | tf_op jit(solution)/shard_map/ppermute | solution.py:313
  83.1 11.4 %copy-start.1 = (bf16[1,1024,256]{2,1,0:T(8,128)(2,1)S(1)}, bf16[1,1024,256]{2,1,0:T(8,128)(2,1)}, u32[]{:S(2)}) copy-start(bf16[1,1024,256]{2,1,0:T(8,128)(2,1)} %param.8) | copy-start | bytes 1572868
  84.9 9.6 %copy-start = (f32[1,1024,256]{2,1,0:T(8,128)S(1)}, f32[1,1024,256]{2,1,0:T(8,128)}, u32[]{:S(2)}) copy-start(f32[1,1024,256]{2,1,0:T(8,128)} %param.9) | copy-start | bytes 3145732
  84.9 9.6 %all-to-all-start.3 = ((bf16[4,32,1024]{2,1,0:T(8,128)(2,1)}), bf16[4,32,1024]{2,1,0:T(8,128)(2,1)S(1)}, u32[]{:S(2)}, u32[]{:S(2)}) async-start(bf16[4,32,1024]{2,1,0:T(8,128)(2,1)} %power.1.after), calls=%async_computation.3 | async-start | bytes 524288 | tf_op jit(solution)/shard_map/all_to_all | solution.py:36
  88.4 1.6 %copy-start.9 = (f32[2560]{0:T(1024)S(1)}, f32[2560]{0:T(1024)}, u32[]{:S(2)}) copy-start(f32[2560]{0:T(1024)} %param.15) | copy-start | bytes 30724
  90.0 0.7 copy-start.8

commit v4 on v3

--- a/solution.py
+++ b/solution.py
@@ -21,7 +21,6 @@
 CHUNKS = 4
 TP = 4
 VMEM = pl.BlockSpec(memory_space=pltpu.VMEM)
-SMEM = pl.BlockSpec(memory_space=pltpu.SMEM)
 ANY = pl.BlockSpec(memory_space=pl.ANY)
 SMALL = pltpu.CompilerParams(vmem_limit_bytes=8 << 20)
 LARGE = pltpu.CompilerParams(vmem_limit_bytes=20 << 20)
@@ -73,42 +72,23 @@
     return lower_inverse(product(left, left, ((1,), (1,)), PRECISE))
 
 
-def quarter_of(place, vector):
+def quarter_of(vector):
     count = vector.shape[0] // TP
-    rows = [vector[place[2] * count + j] for j in range(count)]
+    rows = [vector[lax.axis_index("tp") * count + j] for j in range(count)]
     return jnp.concatenate(rows + [jnp.zeros((8 - count, LANES), F32)], 0)
 
 
-def half_of(side, gradients, feedback, narrow, wide, sems, store):
-    step = gradients.shape[0] // CHUNKS
-    spans = [slice(chunk * step, (chunk + 1) * step) for chunk in range(CHUNKS)]
-    copies = []
-    for chunk, span in enumerate(spans):
-        for which, (source, target) in enumerate(((gradients, narrow), (feedback, wide))):
-            copy = pltpu.make_async_copy(source.at[span, side], target.at[span], sems.at[chunk, which])
-            copy.start()
-            copies.append(copy)
-    for chunk, span in enumerate(spans):
-        copies[2 * chunk].wait()
-        copies[2 * chunk + 1].wait()
-        store(span, narrow[span].astype(F32) + wide[span])
-
-
-def send_kernel(place, gradients, feedback, vector, out, narrow, wide, sems):
-    def store(span, values):
-        out[span] = values.astype(BF16)
-
-    out[gradients.shape[0]] = jnp.concatenate(split(quarter_of(place, vector)), 1)
-    half_of(1 - place[0], gradients, feedback, narrow, wide, sems, store)
-
-
-def keep_kernel(place, gradients, feedback, after, out, narrow, wide, sems):
+def send_kernel(gradients, feedback, vector, out):
+    side = 1 - lax.axis_index("c")
+    chips = gradients.shape[0]
+    out[:chips] = (gradients[:, side].astype(F32) + feedback[:, side]).astype(BF16)
+    out[chips] = jnp.concatenate(split(quarter_of(vector)), 1)
+
+
+def keep_kernel(gradients, feedback, after, out):
     del after
-
-    def store(span, values):
-        out[span] = values
-
-    half_of(place[0], gradients, feedback, narrow, wide, sems, store)
+    side = lax.axis_index("c")
+    out[...] = gradients[:, side].astype(F32) + feedback[:, side]
 
 
 def pair_kernel(kept, received, out):
@@ -120,11 +100,11 @@
     return jnp.concatenate([high.astype(F32), low.astype(F32), jnp.zeros((2, LANES), F32)], 0)
 
 
-def share_kernel(place, arrived, received, vector, momentum, master, out):
+def share_kernel(arrived, received, vector, momentum, master, out):
     total = jnp.sum(arrived[...].astype(F32), axis=0)
     other = received[received.shape[0] - 1].astype(F32)
-    quarter = quarter_of(place, vector) + other[:, :LANES] + other[:, LANES:]
-    rows = jnp.where(place[0] == 0, quarter[0:3], quarter[3:6])
+    quarter = quarter_of(vector) + other[:, :LANES] + other[:, LANES:]
+    rows = jnp.where(lax.axis_index("c") == 0, quarter[0:3], quarter[3:6])
     base = master[...] - LEARN_RATE * MOMENTUM_RATE * momentum[...]
     shared = jnp.concatenate([total, packed_rows(rows), base], 1).astype(BF16)
     out[...] = jnp.broadcast_to(shared, out.shape)
@@ -135,8 +115,8 @@
 
 
 def left_kernel(near, factor, out):
-    cols, _ = factor.shape
-    left = times_exact(factor[...].T, matrix_of(near, cols), ((1,), (1,)))
+    cols = factor.shape[1]
+    left = times_exact(factor[...], matrix_of(near, cols), ((1,), (1,)))
     spread = jnp.sum(near[:, :, cols : cols + LANES].astype(F32), axis=0)
     rows = packed_rows(spread[0:3] + spread[3:6])
     rows = jnp.concatenate([rows, jnp.zeros((8, left.shape[1] - LANES), F32)], 1)
@@ -144,10 +124,10 @@
     out[...] = jnp.broadcast_to(both, out.shape)
 
 
-def left_sum(place, arrived):
+def left_sum(arrived):
     tp = arrived.shape[0] // 2
     rank = arrived.shape[1] - 8
-    core = place[0]
+    core = lax.axis_index("c")
 
     def half(side):
         return jnp.sum(arrived[pl.ds(side * tp, tp), :rank].astype(F32), axis=0)
@@ -155,9 +135,9 @@
     return half(core), half(1 - core)
 
 
-def power_kernel(place, arrived, near, far, out):
+def power_kernel(arrived, near, far, out):
     cols = near.shape[2] * 2 // 5
-    own, other = left_sum(place, arrived)
+    own, other = left_sum(arrived)
     near_matrix, far_matrix = matrix_of(near, cols), matrix_of(far, cols)
     right = times_exact(own, near_matrix, ((1,), (0,))) + times_exact(other, far_matrix, ((1,), (0,)))
     half = own.shape[1]
@@ -166,7 +146,7 @@
         out[:, :, side * half : (side + 1) * half] = jnp.broadcast_to(left, (out.shape[0], *left.shape))
 
 
-def factor_kernel(place, arrived, after, out, vector):
+def factor_kernel(arrived, after, out, vector):
     del after
     peers, filled = arrived.shape[:2]
     tp, rank = peers // 2, filled - 8
@@ -176,12 +156,11 @@
         tile = arrived[peer, rank:, :LANES].astype(F32)
         for row in range(3 if side == 0 else count - 3):
             vector[column * count + 3 * side + row] = tile[row : row + 1] + tile[row + 3 : row + 4]
-    own, other = left_sum(place, arrived)
+    own, other = left_sum(arrived)
     out[...] = gram_inverse(jnp.concatenate([own, other], 1))
 
 
 def finish_kernel(
-    place,
     parts,
     inverse_one,
     near,
@@ -204,7 +183,7 @@
     *,
     replicas,
 ):
-    core, chip = place[0], place[1]
+    core, chip = lax.axis_index("c"), lax.axis_index(CHIPS)
     chips, pair, cols = feedback.shape
     rows = pair // 2
     half = chips * rows
@@ -257,39 +236,31 @@
     replicas = lax.axis_size(REP)
     chips = lax.axis_size(CHIPS)
     tp = lax.axis_size("tp")
-    core = lax.axis_index("c")
     rows, cols = gradients.shape[1:]
     owned = momentum.shape[0]
     rank = warm_factor.shape[1]
     half = rows // 2
-    place = jnp.stack([core, lax.axis_index(CHIPS), lax.axis_index("tp")]).astype(jnp.int32)
     by_pair = (chips, 2 * owned, cols)
     by_owner = (chips, 2, owned, cols)
     lines = vector_grads.reshape(-1, 1, LANES)
     halves = (gradients.reshape(by_owner), feedback.reshape(by_owner))
-    buffers = [
-        pltpu.VMEM((chips, owned, cols), BF16),
-        pltpu.VMEM((chips, owned, cols), F32),
-        pltpu.SemaphoreType.DMA((CHUNKS, 2)),
-    ]
-
     sent = pl.pallas_call(
         send_kernel,
         out_shape=jax.ShapeDtypeStruct((chips + 1, owned, cols), BF16),
-        in_specs=[SMEM, ANY, ANY, VMEM],
-        out_specs=VMEM,
-        scratch_shapes=buffers,
+        in_specs=[VMEM] * 3,
+        out_specs=VMEM,
+        compiler_params=SMALL,
         name="send",
-    )(place, *halves, lines)
+    )(*halves, lines)
     received = lax.ppermute(sent, "c", SWAP)
     kept = pl.pallas_call(
         keep_kernel,
         out_shape=jax.ShapeDtypeStruct((chips, owned, cols), F32),
-        in_specs=[SMEM, ANY, ANY, ANY],
-        out_specs=VMEM,
-        scratch_shapes=buffers,
+        in_specs=[VMEM, VMEM, ANY],
+        out_specs=VMEM,
+        compiler_params=SMALL,
         name="keep",
-    )(place, *halves, sent)
+    )(*halves, sent)
     paired = pl.pallas_call(
         pair_kernel,
         out_shape=jax.ShapeDtypeStruct((chips, owned, cols), BF16),
@@ -304,11 +275,11 @@
     shared = pl.pallas_call(
         share_kernel,
         out_shape=jax.ShapeDtypeStruct((chips, owned, shared_cols), BF16),
-        in_specs=[SMEM] + [VMEM] * 5,
+        in_specs=[VMEM] * 5,
         out_specs=VMEM,
         compiler_params=SMALL,
         name="share",
-    )(place, arrived, received, lines, momentum, master_owned)
+    )(arrived, received, lines, momentum, master_owned)
     near = exchange(shared, CHIPS)
     far = lax.ppermute(near, "c", SWAP)
     left = pl.pallas_call(
@@ -318,24 +289,24 @@
         out_specs=VMEM,
         compiler_params=SMALL,
         name="left",
-    )(near, warm_factor)
+    )(near, warm_factor.T)
     left = exchange(left, ("c", "tp"))
     parts = pl.pallas_call(
         power_kernel,
         out_shape=jax.ShapeDtypeStruct((tp, rank, rows), BF16),
-        in_specs=[SMEM] + [VMEM] * 3,
+        in_specs=[VMEM] * 3,
         out_specs=VMEM,
         compiler_params=SMALL,
         name="power",
-    )(place, left, near, far)
+    )(left, near, far)
     inverse_one, vector = pl.pallas_call(
         factor_kernel,
         out_shape=(jax.ShapeDtypeStruct((rank, rank), F32), jax.ShapeDtypeStruct(lines.shape, F32)),
-        in_specs=[SMEM, VMEM, ANY],
+        in_specs=[VMEM, ANY],
         out_specs=(VMEM, VMEM),
         compiler_params=SMALL,
         name="factor",
-    )(place, left, parts)
+    )(left, parts)
     parts = exchange(parts, "tp")
     vector_sum = vector.reshape(-1)
 
@@ -347,7 +318,7 @@
             jax.ShapeDtypeStruct(momentum.shape, F32),
             jax.ShapeDtypeStruct(momentum.shape, F32),
         ),
-        in_specs=[SMEM] + [VMEM] * 8,
+        in_specs=[VMEM] * 8,
         out_specs=(ANY, ANY, VMEM, VMEM),
         scratch_shapes=[
             pltpu.VMEM((3 * rank, rows), BF16),
@@ -361,7 +332,6 @@
         compiler_params=LARGE,
         name="finish",
     )(
-        place,
         parts,
         inverse_one,
         near,

time: 100 us -> 95.3 us (0.953)
  Pallas kernels: 14 us -> 6.54 us
  local copies, waits for them, and re-layouts: 1.84 us -> 3.66 us
  waiting for transfers between devices: 3.17 us -> 4.77 us
    pallas_call x1, Pallas kernels: 2.76 us -> 0.07 us  [shards(): pl.pallas_call(keep_kernel, out_shape=jax.ShapeDtypeStruct((chips, owned,...]
    pallas_call x1, Pallas kernels: 2.71 us -> 0.06 us  [shards(): pl.pallas_call(send_kernel, out_shape=jax.ShapeDtypeStruct((chips + 1, ow...]
    unnamed x21 -> x22, local copies, waits for them, and re-layouts: 1.84 us -> 3.66 us
    ppermute x1, waiting for transfers between devices: 0.01 us -> 1.07 us  [shards(): received = lax.ppermute(sent, 'c', SWAP)]
  transfers between devices with their start and end apart: 3 -> 3, of which waited for: 1 -> 2; matrix products, arithmetic and copies ran while one was open for 1% -> 1% of each run, Pallas kernels for 5% -> 1%
where the time goes in v4:
time: 95.3 us; the launch traced here: 94.1 us
  blocking collectives  59.5 us (62%)
  starting transfers between devices  18.1 us (19%)
  Pallas kernels  6.54 us (7%)
  waiting for transfers between devices  4.77 us (5%)
  local copies, waits for them, and re-layouts  3.66 us (4%)
    all_to_all x3, blocking collectives, exchange(): return lax.all_to_all(array, axis, 0, 0, tiled=True)  59.5 us
    ppermute x1, starting transfers between devices, shards(): received = lax.ppermute(sent, 'c', SWAP)  8.75 us
    ppermute x1, starting transfers between devices, shards(): far = lax.ppermute(near, 'c', SWAP)  5.85 us
    pallas_call x1, Pallas kernels, shards(): pl.pallas_call(functools.partial(finish_kernel, replicas=replicas), out_s...  3.77 us
    all_to_all x1, waiting for transfers between devices, exchange(): return lax.all_to_all(array, axis, 0, 0, tiled=True)  3.7 us
    unnamed x22, local copies, waits for them, and re-layouts  3.66 us
    all_to_all x1, starting transfers between devices, exchange(): return lax.all_to_all(array, axis, 0, 0, tiled=True)  3.54 us
  transfers between devices with their start and end apart: 3, of which 2 were waited for; matrix products, arithmetic and copies ran while one was open for 1% of the time, Pallas kernels for 1%

profile of v4, /device:TPU:1, one launch (start us, length us, event | category | flops | bytes accessed | tf_op | source)
XLA Modules:
  0.0 94.1 jit_solution(12597390004090533549)
XLA Ops:
  0.6 0.0 copy-start
  0.6 1.2 %copy-done = f32[1,1024,256]{2,1,0:T(8,128)S(1)} copy-done((f32[1,1024,256]{2,1,0:T(8,128)S(1)}, f32[1,1024,256]{2,1,0:T(8,128)}, u32[]{:S(2)}) %copy-start) | copy-done | bytes 1048600
  1.9 1.0 %copy-done.2 = bf16[1,1024,256]{2,1,0:T(8,128)(2,1)S(1)} copy-done((bf16[1,1024,256]{2,1,0:T(8,128)(2,1)S(1)}, bf16[1,1024,256]{2,1,0:T(8,128)(2,1)}, u32[]{:S(2)}) %copy-start.2) | copy-done | bytes 524312
  2.9 0.7 copy-done.4
  3.6 0.1 send.1.after
  3.7 8.8 %collective-permute-start = (bf16[65,8,256]{2,1,0:T(8,128)(2,1)S(1)}, bf16[65,8,256]{2,1,0:T(8,128)(2,1)S(1)}, u32[]{:S(2)}, u32[]{:S(2)}) collective-permute-start(bf16[65,8,256]{2,1,0:T(8,128)(2,1)S(1)} %send.1.after), channel_id=1, source_target_pairs={{0,4},{4,0},{1,5},{5,1},{2,6},{6,2},{3,7},{7,3},{8,12},{12,8},{9,1... | collective-permute-start | bytes 798728 | tf_op jit(solution)/shard_map/ppermute | solution.py:255
  12.4 0.1 keep.1.kept
  12.5 1.1 %collective-permute-done.received = bf16[65,8,256]{2,1,0:T(8,128)(2,1)S(1)} collective-permute-done((bf16[65,8,256]{2,1,0:T(8,128)(2,1)S(1)}, bf16[65,8,256]{2,1,0:T(8,128)(2,1)S(1)}, u32[]{:S(2)}, u32[]{:S(2)}) %collective-permute-start) | collective-permute-done | bytes 266272 | tf_op jit(solution)/shard_map/ppermute | solution.py:255
  13.6 0.1 pair.1
  13.6 0.0 copy-start.5
  13.6 0.0 copy-start.6
  13.7 0.0 copy-start.7
  13.7 24.0 %all_to_all.20.arrived = bf16[64,8,256]{2,1,0:T(8,128)(2,1)S(1)} all-to-all(bf16[64,8,256]{2,1,0:T(8,128)(2,1)S(1)} %pair.1), channel_id=1, replica_groups=mesh['y'=8,'z'=8,'c'=2,'tp'=4] {'y','z'}, dimensions={0} | all-to-all | bytes 524288 | tf_op jit(solution)/shard_map/all_to_all | solution.py:35
  37.6 0.0 copy-done.5
  37.6 0.0 copy-done.6
  37.6 0.0 copy-done.7
  37.6 0.1 share.1
  37.8 0.0 copy-start.8
  37.8 23.8 %all_to_all.21.near = bf16[64,8,640]{2,1,0:T(8,128)(2,1)S(1)} all-to-all(bf16[64,8,640]{2,1,0:T(8,128)(2,1)S(1)} %share.1), channel_id=1, replica_groups=mesh['y'=8,'z'=8,'c'=2,'tp'=4] {'y','z'}, dimensions={0} | all-to-all | bytes 1310720 | tf_op jit(solution)/shard_map/all_to_all | solution.py:35
  61.6 5.9 %collective-permute-start.1 = (bf16[64,8,640]{2,1,0:T(8,128)(2,1)S(1)}, bf16[64,8,640]{2,1,0:T(8,128)(2,1)S(1)}, u32[]{:S(2)}, u32[]{:S(2)}) collective-permute-start(bf16[64,8,640]{2,1,0:T(8,128)(2,1)S(1)} %all_to_all.21.near), channel_id=1, source_target_pairs={{0,4},{4,0},{1,5},{5,1},{2,6},{6,2},{3,7},{7,3},{8,12},{12,8},{9,1... | collective-permute-start | bytes 1966088 | tf_op jit(solution)/shard_map/ppermute | solution.py:284
  67.4 0.2 left.1
  67.7 11.8 %all_to_all.22.arrived = bf16[8,40,512]{2,1,0:T(8,128)(2,1)S(1)} all-to-all(bf16[8,40,512]{2,1,0:T(8,128)(2,1)S(1)} %left.1), channel_id=1, replica_groups=mesh['y'=8,'z'=8,'c'=2,'tp'=4] {'c','tp'}, dimensions={0} | all-to-all | bytes 655360 | tf_op jit(solution)/shard_map/all_to_all | solution.py:35
  79.4 0.0 collective-permute-done.1.far
  79.4 1.3 %power.1.after = bf16[4,32,1024]{2,1,0:T(8,128)(2,1)} custom-call(bf16[8,40,512]{2,1,0:T(8,128)(2,1)S(1)} %all_to_all.22.arrived, bf16[64,8,640]{2,1,0:T(8,128)(2,1)S(1)} %all_to_all.21.near, bf16[64,8,640]{2,1,0:T(8,128)(2,1)S(1)} %collective-permute-done.1.far), custom_call_target="tpu_custom_call" | custom-call | tf_op jit(solution)/shard_map/power/pallas_call | solution.py:294
  80.7 3.5 %all-to-all-start.3 = ((bf16[4,32,1024]{2,1,0:T(8,128)(2,1)}), bf16[4,32,1024]{2,1,0:T(8,128)(2,1)S(1)}, u32[]{:S(2)}, u32[]{:S(2)}) async-start(bf16[4,32,1024]{2,1,0:T(8,128)(2,1)} %power.1.after), calls=%async_computation.3 | async-start | bytes 524288 | tf_op jit(solution)/shard_map/all_to_all | solution.py:35
  84.2 0.0 copy-start.10
  84.3 1.0 %factor.1 = (f32[32,32]{1,0:T(8,128)S(1)}, f32[20,1,128]{2,1,0:T(1,128)S(1)}) custom-call(bf16[8,40,512]{2,1,0:T(8,128)(2,1)S(1)} %all_to_all.22.arrived, bf16[4,32,1024]{2,1,0:T(8,128)(2,1)} %power.1.after), custom_call_target="tpu_custom_call" | custom-call | tf_op jit(solution)/shard_map/factor/pallas_call | solution.py:302
  85.3 0.7 copy-done.9
  86.0 0.6 multiply_subtract_fusion
  86.6 3.7 %all-to-all-done.3.parts = bf16[4,32,1024]{2,1,0:T(8,128)(2,1)S(1)} async-done(((bf16[4,32,1024]{2,1,0:T(8,128)(2,1)}), bf16[4,32,1024]{2,1,0:T(8,128)(2,1)S(1)}, u32[]{:S(2)}, u32[]{:S(2)}) %all-to-all-start.3) | async-done | bytes 262176 | tf_op jit(solution)/shard_map/all_to_all | solution.py:35
  90.3 0.0 copy-done.3
  90.3 3.8 %finish.1 = (f32[64,16,256]{2,1,0:T(8,128)}, bf16[64,16,256]{2,1,0:T(8,128)(2,1)}, f32[8,256]{1,0:T(8,128)}, f32[8,256]{1,0:T(8,128)}) custom-call(bf16[4,32,1024]{2,1,0:T(8,128)(2,1)S(1)} %all-to-all-done.3.parts, f32[32,32]{1,0:T(8,128)S(1)} %get-tuple-element.12.inverse_one, bf16[64,8,640]{2,1,0:T(8,128)(2,1)S(1)} %all_to_all.21.near, ...), custom_call_target="tpu_custom_call" | custom-call | tf_op jit(solution)/shard_map/finish/pallas_call | solution.py:313
  (9 shorter events, 0.1 us)
Async XLA Ops:
  0.6 1.2 %copy-start = (f32[1,1024,256]{2,1,0:T(8,128)S(1)}, f32[1,1024,256]{2,1,0:T(8,128)}, u32[]{:S(2)}) copy-start(f32[1,1024,256]{2,1,0:T(8,128)} %param.9) | copy-start | bytes 3145732
  1.9 1.0 %copy-start.2 = (bf16[1,1024,256]{2,1,0:T(8,128)(2,1)S(1)}, bf16[1,1024,256]{2,1,0:T(8,128)(2,1)}, u32[]{:S(2)}) copy-start(bf16[1,1024,256]{2,1,0:T(8,128)(2,1)} %param.8) | copy-start | bytes 1572868
  2.9 0.7 copy-start.4
  3.7 9.9 %collective-permute-start = (bf16[65,8,256]{2,1,0:T(8,128)(2,1)S(1)}, bf16[65,8,256]{2,1,0:T(8,128)(2,1)S(1)}, u32[]{:S(2)}, u32[]{:S(2)}) collective-permute-start(bf16[65,8,256]{2,1,0:T(8,128)(2,1)S(1)} %send.1.after), channel_id=1, source_target_pairs={{0,4},{4,0},{1,5},{5,1},{2,6},{6,2},{3,7},{7,3},{8,12},{12,8},{9,1... | collective-permute-start | bytes 798728 | tf_op jit(solution)/shard_map/ppermute | solution.py:255
  13.6 24.0 %copy-start.5 = (f32[1,2560]{1,0:T(1,128)S(1)}, f32[1,2560]{1,0:T(1,128)}, u32[]{:S(2)}) copy-start(f32[1,2560]{1,0:T(1,128)} %param.13) | copy-start | bytes 30724
  13.6 24.0 %copy-start.6 = (f32[8,256]{1,0:T(8,128)S(1)}, f32[8,256]{1,0:T(8,128)}, u32[]{:S(2)}) copy-start(f32[8,256]{1,0:T(8,128)} %momentum.3) | copy-start | bytes 24580
  13.7 24.0 %copy-start.7 = (f32[8,256]{1,0:T(8,128)S(1)}, f32[8,256]{1,0:T(8,128)}, u32[]{:S(2)}) copy-start(f32[8,256]{1,0:T(8,128)} %master.3) | copy-start | bytes 24580
  37.8 29.7 %copy-start.8 = (f32[256,32]{0,1:T(8,128)S(1)}, f32[256,32]{0,1:T(8,128)}, u32[]{:S(2)}) copy-start(f32[256,32]{0,1:T(8,128)} %param.10) | copy-start | bytes 98308
  61.6 17.9 %collective-permute-start.1 = (bf16[64,8,640]{2,1,0:T(8,128)(2,1)S(1)}, bf16[64,8,640]{2,1,0:T(8,128)(2,1)S(1)}, u32[]{:S(2)}, u32[]{:S(2)}) collective-permute-start(bf16[64,8,640]{2,1,0:T(8,128)(2,1)S(1)} %all_to_all.21.near), channel_id=1, source_target_pairs={{0,4},{4,0},{1,5},{5,1},{2,6},{6,2},{3,7},{7,3},{8,12},{12,8},{9,1... | collective-permute-start | bytes 1966088 | tf_op jit(solution)/shard_map/ppermute | solution.py:284
  79.4 10.9 %copy-start.3 = (bf16[1,1024,256]{2,1,0:T(8,128)(2,1)S(1)}, bf16[1,1024,256]{2,1,0:T(8,128)(2,1)}, u32[]{:S(2)}) copy-start(bf16[1,1024,256]{2,1,0:T(8,128)(2,1)} %param.8) | copy-start | bytes 1572868
  80.7 9.6 %copy-start.1 = (f32[1,1024,256]{2,1,0:T(8,128)S(1)}, f32[1,1024,256]{2,1,0:T(8,128)}, u32[]{:S(2)}) copy-start(f32[1,1024,256]{2,1,0:T(8,128)} %param.9) | copy-start | bytes 3145732
  80.7 9.6 %all-to-all-start.3 = ((bf16[4,32,1024]{2,1,0:T(8,128)(2,1)}), bf16[4,32,1024]{2,1,0:T(8,128)(2,1)S(1)}, u32[]{:S(2)}, u32[]{:S(2)}) async-start(bf16[4,32,1024]{2,1,0:T(8,128)(2,1)} %power.1.after), calls=%async_computation.3 | async-start | bytes 524288 | tf_op jit(solution)/shard_map/all_to_all | solution.py:35
  84.2 1.1 %copy-start.10 = (f32[2560]{0:T(1024)S(1)}, f32[2560]{0:T(1024)}, u32[]{:S(2)}) copy-start(f32[2560]{0:T(1024)} %param.15) | copy-start | bytes 30724
  85.3 0.7 copy-start.9

commit v5 on v4

--- a/solution.py
+++ b/solution.py
@@ -23,6 +23,7 @@
 VMEM = pl.BlockSpec(memory_space=pltpu.VMEM)
 ANY = pl.BlockSpec(memory_space=pl.ANY)
 SMALL = pltpu.CompilerParams(vmem_limit_bytes=8 << 20)
+PACK = pltpu.CompilerParams(vmem_limit_bytes=54400 << 10)
 LARGE = pltpu.CompilerParams(vmem_limit_bytes=20 << 20)
 
 
@@ -78,17 +79,25 @@
     return jnp.concatenate(rows + [jnp.zeros((8 - count, LANES), F32)], 0)
 
 
-def send_kernel(gradients, feedback, vector, out):
-    side = 1 - lax.axis_index("c")
+def pack_kernel(gradients, feedback, vector, sent, kept, narrow, wide, line, sems):
+    core = lax.axis_index("c")
     chips = gradients.shape[0]
-    out[:chips] = (gradients[:, side].astype(F32) + feedback[:, side]).astype(BF16)
-    out[chips] = jnp.concatenate(split(quarter_of(vector)), 1)
-
-
-def keep_kernel(gradients, feedback, after, out):
-    del after
-    side = lax.axis_index("c")
-    out[...] = gradients[:, side].astype(F32) + feedback[:, side]
+    step = chips // CHUNKS
+    spans = [slice(chunk * step, (chunk + 1) * step) for chunk in range(CHUNKS)]
+    last = pltpu.make_async_copy(vector, line, sems.at[CHUNKS, 0])
+    copies = []
+    for chunk, span in enumerate(spans):
+        pair = ((gradients, narrow), (feedback, wide))
+        copies += [pltpu.make_async_copy(s.at[span], t.at[span], sems.at[chunk, w]) for w, (s, t) in enumerate(pair)]
+    for copy in (*copies, last):
+        copy.start()
+    for chunk, span in enumerate(spans):
+        copies[2 * chunk].wait()
+        copies[2 * chunk + 1].wait()
+        sent[span] = (narrow[span, 1 - core].astype(F32) + wide[span, 1 - core]).astype(BF16)
+        kept[span] = narrow[span, core].astype(F32) + wide[span, core]
+    last.wait()
+    sent[chips] = jnp.concatenate(split(quarter_of(line)), 1)
 
 
 def pair_kernel(kept, received, out):
@@ -244,23 +253,24 @@
     by_owner = (chips, 2, owned, cols)
     lines = vector_grads.reshape(-1, 1, LANES)
     halves = (gradients.reshape(by_owner), feedback.reshape(by_owner))
-    sent = pl.pallas_call(
-        send_kernel,
-        out_shape=jax.ShapeDtypeStruct((chips + 1, owned, cols), BF16),
-        in_specs=[VMEM] * 3,
-        out_specs=VMEM,
-        compiler_params=SMALL,
-        name="send",
+    sent, kept = pl.pallas_call(
+        pack_kernel,
+        out_shape=(
+            jax.ShapeDtypeStruct((chips + 1, owned, cols), BF16),
+            jax.ShapeDtypeStruct((chips, owned, cols), F32),
+        ),
+        in_specs=[ANY] * 3,
+        out_specs=(VMEM, VMEM),
+        scratch_shapes=[
+            pltpu.VMEM(by_owner, BF16),
+            pltpu.VMEM(by_owner, F32),
+            pltpu.VMEM(lines.shape, F32),
+            pltpu.SemaphoreType.DMA((CHUNKS + 1, 2)),
+        ],
+        compiler_params=PACK,
+        name="pack",
     )(*halves, lines)
     received = lax.ppermute(sent, "c", SWAP)
-    kept = pl.pallas_call(
-        keep_kernel,
-        out_shape=jax.ShapeDtypeStruct((chips, owned, cols), F32),
-        in_specs=[VMEM, VMEM, ANY],
-        out_specs=VMEM,
-        compiler_params=SMALL,
-        name="keep",
-    )(*halves, sent)
     paired = pl.pallas_call(
         pair_kernel,
         out_shape=jax.ShapeDtypeStruct((chips, owned, cols), BF16),

time: 95.3 us -> 94.3 us (0.990)
  local copies, waits for them, and re-layouts: 3.66 us -> 1.39 us
  Pallas kernels: 6.54 us -> 7.92 us
    unnamed x22 -> x16, local copies, waits for them, and re-layouts: 3.66 us -> 1.39 us
    pallas_call x2 -> x1, Pallas kernels: 0.13 us -> 1.52 us  [shards(): pl.pallas_call(pack_kernel, out_shape=(jax.ShapeDtypeStruct((chips + 1, o...]
where the time goes in v5:
time: 94.3 us; the launch traced here: 93.1 us
  blocking collectives  59.4 us (63%)
  starting transfers between devices  18.1 us (19%)
  Pallas kernels  7.92 us (8%)
  waiting for transfers between devices  4.85 us (5%)
  local copies, waits for them, and re-layouts  1.39 us (1%)
    all_to_all x3, blocking collectives, exchange(): return lax.all_to_all(array, axis, 0, 0, tiled=True)  59.4 us
    ppermute x1, starting transfers between devices, shards(): received = lax.ppermute(sent, 'c', SWAP)  8.75 us
    ppermute x1, starting transfers between devices, shards(): far = lax.ppermute(near, 'c', SWAP)  5.85 us
    pallas_call x1, Pallas kernels, shards(): pl.pallas_call(functools.partial(finish_kernel, replicas=replicas), out_s...  3.77 us
    all_to_all x1, waiting for transfers between devices, exchange(): return lax.all_to_all(array, axis, 0, 0, tiled=True)  3.7 us
    all_to_all x1, starting transfers between devices, exchange(): return lax.all_to_all(array, axis, 0, 0, tiled=True)  3.54 us
  transfers between devices with their start and end apart: 3, of which 2 were waited for; matrix products, arithmetic and copies ran while one was open for 1% of the time, Pallas kernels for 1%

profile of v5, /device:TPU:1, one launch (start us, length us, event | category | flops | bytes accessed | tf_op | source)
XLA Modules:
  0.0 93.1 jit_solution(7241091560421945902)
XLA Ops:
  0.6 0.0 copy-start.2
  0.6 0.7 copy-done.2
  1.3 1.5 %pack.1 = (bf16[65,8,256]{2,1,0:T(8,128)(2,1)S(1)}, f32[64,8,256]{2,1,0:T(8,128)S(1)}) custom-call(bf16[64,2,8,256]{3,2,1,0:T(8,128)(2,1)} %bitcast.13, f32[64,2,8,256]{3,2,1,0:T(8,128)} %bitcast.11, f32[20,1,128]{2,1,0:T(1,128)S(1)} %bitcast.15), custom_call_target="tpu_custom_call" | custom-call | tf_op jit(solution)/shard_map/pack/pallas_call | solution.py:256
  2.9 8.8 %collective-permute-start = (bf16[65,8,256]{2,1,0:T(8,128)(2,1)S(1)}, bf16[65,8,256]{2,1,0:T(8,128)(2,1)S(1)}, u32[]{:S(2)}, u32[]{:S(2)}) collective-permute-start(bf16[65,8,256]{2,1,0:T(8,128)(2,1)S(1)} %get-tuple-element.15), channel_id=1, source_target_pairs={{0,4},{4,0},{1,5},{5,1},{2,6},{6,2},{3,7},{7,3},{8,12},{12,8},{9,1... | collective-permute-start | bytes 798728 | tf_op jit(solution)/shard_map/ppermute | solution.py:273
  11.6 1.1 %collective-permute-done.received = bf16[65,8,256]{2,1,0:T(8,128)(2,1)S(1)} collective-permute-done((bf16[65,8,256]{2,1,0:T(8,128)(2,1)S(1)}, bf16[65,8,256]{2,1,0:T(8,128)(2,1)S(1)}, u32[]{:S(2)}, u32[]{:S(2)}) %collective-permute-start) | collective-permute-done | bytes 266272 | tf_op jit(solution)/shard_map/ppermute | solution.py:273
  12.8 0.0 copy-start.3
  12.8 0.0 copy-start.4
  12.8 23.8 %all_to_all.20.arrived = bf16[64,8,256]{2,1,0:T(8,128)(2,1)S(1)} all-to-all(bf16[64,8,256]{2,1,0:T(8,128)(2,1)S(1)} %pair.1), channel_id=1, replica_groups=mesh['y'=8,'z'=8,'c'=2,'tp'=4] {'y','z'}, dimensions={0} | all-to-all | bytes 524288 | tf_op jit(solution)/shard_map/all_to_all | solution.py:36
  36.7 0.0 copy-done.3
  36.7 0.0 copy-done.4
  36.7 0.1 share.1
  36.8 0.0 copy-start.5
  36.8 23.8 %all_to_all.21.near = bf16[64,8,640]{2,1,0:T(8,128)(2,1)S(1)} all-to-all(bf16[64,8,640]{2,1,0:T(8,128)(2,1)S(1)} %share.1), channel_id=1, replica_groups=mesh['y'=8,'z'=8,'c'=2,'tp'=4] {'y','z'}, dimensions={0} | all-to-all | bytes 1310720 | tf_op jit(solution)/shard_map/all_to_all | solution.py:36
  60.6 5.9 %collective-permute-start.1 = (bf16[64,8,640]{2,1,0:T(8,128)(2,1)S(1)}, bf16[64,8,640]{2,1,0:T(8,128)(2,1)S(1)}, u32[]{:S(2)}, u32[]{:S(2)}) collective-permute-start(bf16[64,8,640]{2,1,0:T(8,128)(2,1)S(1)} %all_to_all.21.near), channel_id=1, source_target_pairs={{0,4},{4,0},{1,5},{5,1},{2,6},{6,2},{3,7},{7,3},{8,12},{12,8},{9,1... | collective-permute-start | bytes 1966088 | tf_op jit(solution)/shard_map/ppermute | solution.py:294
  66.5 0.0 copy-done.5
  66.5 0.2 left.1
  66.7 11.8 %all_to_all.22.arrived = bf16[8,40,512]{2,1,0:T(8,128)(2,1)S(1)} all-to-all(bf16[8,40,512]{2,1,0:T(8,128)(2,1)S(1)} %left.1), channel_id=1, replica_groups=mesh['y'=8,'z'=8,'c'=2,'tp'=4] {'c','tp'}, dimensions={0} | all-to-all | bytes 655360 | tf_op jit(solution)/shard_map/all_to_all | solution.py:36
  78.5 0.0 collective-permute-done.1.far
  78.5 0.0 copy-start.1
  78.5 1.3 %power.1.after = bf16[4,32,1024]{2,1,0:T(8,128)(2,1)} custom-call(bf16[8,40,512]{2,1,0:T(8,128)(2,1)S(1)} %all_to_all.22.arrived, bf16[64,8,640]{2,1,0:T(8,128)(2,1)S(1)} %all_to_all.21.near, bf16[64,8,640]{2,1,0:T(8,128)(2,1)S(1)} %collective-permute-done.1.far), custom_call_target="tpu_custom_call" | custom-call | tf_op jit(solution)/shard_map/power/pallas_call | solution.py:304
  79.7 0.0 copy-start
  79.7 3.5 %all-to-all-start.3 = ((bf16[4,32,1024]{2,1,0:T(8,128)(2,1)}), bf16[4,32,1024]{2,1,0:T(8,128)(2,1)S(1)}, u32[]{:S(2)}, u32[]{:S(2)}) async-start(bf16[4,32,1024]{2,1,0:T(8,128)(2,1)} %power.1.after), calls=%async_computation.3 | async-start | bytes 524288 | tf_op jit(solution)/shard_map/all_to_all | solution.py:36
  83.3 0.0 copy-start.7
  83.3 1.0 %factor.1 = (f32[32,32]{1,0:T(8,128)S(1)}, f32[20,1,128]{2,1,0:T(1,128)S(1)}) custom-call(bf16[8,40,512]{2,1,0:T(8,128)(2,1)S(1)} %all_to_all.22.arrived, bf16[4,32,1024]{2,1,0:T(8,128)(2,1)} %power.1.after), custom_call_target="tpu_custom_call" | custom-call | tf_op jit(solution)/shard_map/factor/pallas_call | solution.py:312
  84.3 0.0 copy-start.6
  84.3 0.0 copy-done.7
  84.4 0.7 copy-done.6
  85.0 0.6 multiply_subtract_fusion
  85.6 3.7 %all-to-all-done.3.parts = bf16[4,32,1024]{2,1,0:T(8,128)(2,1)S(1)} async-done(((bf16[4,32,1024]{2,1,0:T(8,128)(2,1)}), bf16[4,32,1024]{2,1,0:T(8,128)(2,1)S(1)}, u32[]{:S(2)}, u32[]{:S(2)}) %all-to-all-start.3) | async-done | bytes 262176 | tf_op jit(solution)/shard_map/all_to_all | solution.py:36
  89.3 0.0 copy-done.1
  89.3 0.0 copy-done
  89.3 3.8 %finish.1 = (f32[64,16,256]{2,1,0:T(8,128)}, bf16[64,16,256]{2,1,0:T(8,128)(2,1)}, f32[8,256]{1,0:T(8,128)}, f32[8,256]{1,0:T(8,128)}) custom-call(bf16[4,32,1024]{2,1,0:T(8,128)(2,1)S(1)} %all-to-all-done.3.parts, f32[32,32]{1,0:T(8,128)S(1)} %get-tuple-element.16.inverse_one, bf16[64,8,640]{2,1,0:T(8,128)(2,1)S(1)} %all_to_all.21.near, ...), custom_call_target="tpu_custom_call" | custom-call | tf_op jit(solution)/shard_map/finish/pallas_call | solution.py:323
  (2 shorter events, 0.1 us)
Async XLA Ops:
  0.6 0.7 copy-start.2
  2.9 9.9 %collective-permute-start = (bf16[65,8,256]{2,1,0:T(8,128)(2,1)S(1)}, bf16[65,8,256]{2,1,0:T(8,128)(2,1)S(1)}, u32[]{:S(2)}, u32[]{:S(2)}) collective-permute-start(bf16[65,8,256]{2,1,0:T(8,128)(2,1)S(1)} %get-tuple-element.15), channel_id=1, source_target_pairs={{0,4},{4,0},{1,5},{5,1},{2,6},{6,2},{3,7},{7,3},{8,12},{12,8},{9,1... | collective-permute-start | bytes 798728 | tf_op jit(solution)/shard_map/ppermute | solution.py:273
  12.8 23.9 %copy-start.3 = (f32[8,256]{1,0:T(8,128)S(1)}, f32[8,256]{1,0:T(8,128)}, u32[]{:S(2)}) copy-start(f32[8,256]{1,0:T(8,128)} %momentum.3) | copy-start | bytes 24580
  12.8 23.9 %copy-start.4 = (f32[8,256]{1,0:T(8,128)S(1)}, f32[8,256]{1,0:T(8,128)}, u32[]{:S(2)}) copy-start(f32[8,256]{1,0:T(8,128)} %master.3) | copy-start | bytes 24580
  36.8 29.7 %copy-start.5 = (f32[256,32]{0,1:T(8,128)S(1)}, f32[256,32]{0,1:T(8,128)}, u32[]{:S(2)}) copy-start(f32[256,32]{0,1:T(8,128)} %param.10) | copy-start | bytes 98308
  60.6 17.9 %collective-permute-start.1 = (bf16[64,8,640]{2,1,0:T(8,128)(2,1)S(1)}, bf16[64,8,640]{2,1,0:T(8,128)(2,1)S(1)}, u32[]{:S(2)}, u32[]{:S(2)}) collective-permute-start(bf16[64,8,640]{2,1,0:T(8,128)(2,1)S(1)} %all_to_all.21.near), channel_id=1, source_target_pairs={{0,4},{4,0},{1,5},{5,1},{2,6},{6,2},{3,7},{7,3},{8,12},{12,8},{9,1... | collective-permute-start | bytes 1966088 | tf_op jit(solution)/shard_map/ppermute | solution.py:294
  78.5 10.9 %copy-start.1 = (bf16[1,1024,256]{2,1,0:T(8,128)(2,1)S(1)}, bf16[1,1024,256]{2,1,0:T(8,128)(2,1)}, u32[]{:S(2)}) copy-start(bf16[1,1024,256]{2,1,0:T(8,128)(2,1)} %param.8) | copy-start | bytes 1572868
  79.7 9.6 %copy-start = (f32[1,1024,256]{2,1,0:T(8,128)S(1)}, f32[1,1024,256]{2,1,0:T(8,128)}, u32[]{:S(2)}) copy-start(f32[1,1024,256]{2,1,0:T(8,128)} %param.9) | copy-start | bytes 3145732
  79.7 9.6 %all-to-all-start.3 = ((bf16[4,32,1024]{2,1,0:T(8,128)(2,1)}), bf16[4,32,1024]{2,1,0:T(8,128)(2,1)S(1)}, u32[]{:S(2)}, u32[]{:S(2)}) async-start(bf16[4,32,1024]{2,1,0:T(8,128)(2,1)} %power.1.after), calls=%async_computation.3 | async-start | bytes 524288 | tf_op jit(solution)/shard_map/all_to_all | solution.py:36
  83.3 1.1 %copy-start.7 = (f32[2560]{0:T(1024)S(1)}, f32[2560]{0:T(1024)}, u32[]{:S(2)}) copy-start(f32[2560]{0:T(1024)} %param.15) | copy-start | bytes 30724
  84.3 0.7 copy-start.6

commit v6 on v5

--- a/solution.py
+++ b/solution.py
@@ -18,7 +18,7 @@
 SWAP = ((0, 1), (1, 0))
 LANES = 128
 PIVOTS = 8
-CHUNKS = 4
+CHUNKS = 2
 TP = 4
 VMEM = pl.BlockSpec(memory_space=pltpu.VMEM)
 ANY = pl.BlockSpec(memory_space=pl.ANY)
@@ -79,43 +79,32 @@
     return jnp.concatenate(rows + [jnp.zeros((8 - count, LANES), F32)], 0)
 
 
-def pack_kernel(gradients, feedback, vector, sent, kept, narrow, wide, line, sems):
+def pack_kernel(gradients, feedback, sent, kept, narrow, wide, sems):
     core = lax.axis_index("c")
     chips = gradients.shape[0]
     step = chips // CHUNKS
     spans = [slice(chunk * step, (chunk + 1) * step) for chunk in range(CHUNKS)]
-    last = pltpu.make_async_copy(vector, line, sems.at[CHUNKS, 0])
     copies = []
     for chunk, span in enumerate(spans):
         pair = ((gradients, narrow), (feedback, wide))
         copies += [pltpu.make_async_copy(s.at[span], t.at[span], sems.at[chunk, w]) for w, (s, t) in enumerate(pair)]
-    for copy in (*copies, last):
+    for copy in copies:
         copy.start()
     for chunk, span in enumerate(spans):
         copies[2 * chunk].wait()
         copies[2 * chunk + 1].wait()
         sent[span] = (narrow[span, 1 - core].astype(F32) + wide[span, 1 - core]).astype(BF16)
         kept[span] = narrow[span, core].astype(F32) + wide[span, core]
-    last.wait()
-    sent[chips] = jnp.concatenate(split(quarter_of(line)), 1)
 
 
 def pair_kernel(kept, received, out):
-    out[...] = (kept[...] + received[: kept.shape[0]].astype(F32)).astype(BF16)
-
-
-def packed_rows(rows):
-    high, low = split(rows)
-    return jnp.concatenate([high.astype(F32), low.astype(F32), jnp.zeros((2, LANES), F32)], 0)
-
-
-def share_kernel(arrived, received, vector, momentum, master, out):
+    out[...] = (kept[...] + received[...].astype(F32)).astype(BF16)
+
+
+def share_kernel(arrived, vector, momentum, master, out):
     total = jnp.sum(arrived[...].astype(F32), axis=0)
-    other = received[received.shape[0] - 1].astype(F32)
-    quarter = quarter_of(vector) + other[:, :LANES] + other[:, LANES:]
-    rows = jnp.where(lax.axis_index("c") == 0, quarter[0:3], quarter[3:6])
     base = master[...] - LEARN_RATE * MOMENTUM_RATE * momentum[...]
-    shared = jnp.concatenate([total, packed_rows(rows), base], 1).astype(BF16)
+    shared = jnp.concatenate([total, quarter_of(vector), base], 1).astype(BF16)
     out[...] = jnp.broadcast_to(shared, out.shape)
 
 
@@ -126,9 +115,9 @@
 def left_kernel(near, factor, out):
     cols = factor.shape[1]
     left = times_exact(factor[...], matrix_of(near, cols), ((1,), (1,)))
-    spread = jnp.sum(near[:, :, cols : cols + LANES].astype(F32), axis=0)
-    rows = packed_rows(spread[0:3] + spread[3:6])
-    rows = jnp.concatenate([rows, jnp.zeros((8, left.shape[1] - LANES), F32)], 1)
+    high, low = split(jnp.sum(near[:, :, cols : cols + LANES].astype(F32), axis=0))
+    blank = jnp.zeros((8, left.shape[1] - 2 * LANES), F32)
+    rows = jnp.concatenate([high.astype(F32), low.astype(F32), blank], 1)
     both = jnp.concatenate([left, rows], 0).astype(BF16)
     out[...] = jnp.broadcast_to(both, out.shape)
 
@@ -160,11 +149,11 @@
     peers, filled = arrived.shape[:2]
     tp, rank = peers // 2, filled - 8
     count = vector.shape[0] // tp
-    for peer in range(peers):
-        side, column = peer // tp, peer % tp
-        tile = arrived[peer, rank:, :LANES].astype(F32)
-        for row in range(3 if side == 0 else count - 3):
-            vector[column * count + 3 * side + row] = tile[row : row + 1] + tile[row + 3 : row + 4]
+    for column in range(tp):
+        tiles = arrived[column, rank:].astype(F32) + arrived[tp + column, rank:].astype(F32)
+        tile = tiles[:, :LANES] + tiles[:, LANES : 2 * LANES]
+        for row in range(count):
+            vector[column * count + row] = tile[row : row + 1]
     own, other = left_sum(arrived)
     out[...] = gram_inverse(jnp.concatenate([own, other], 1))
 
@@ -207,24 +196,17 @@
     for side, start in enumerate((core * half, (1 - core) * half)):
         high, low = split(ortho[:, side * half : (side + 1) * half])
         ortho_terms[:, pl.ds(pl.multiple_of(start, LANES), half)] = jnp.concatenate([high, high, low], 0)
-    step = chips // CHUNKS
-    copies = []
-    for chunk in range(CHUNKS):
-        span = slice(chunk * step, (chunk + 1) * step)
-        sides = []
-        for side in range(2):
-            at = side * half + chunk * step * rows
-            terms = ortho_terms[:, at : at + step * rows]
-            sides.append(product(terms, right_terms[...], ((0,), (0,))).reshape(step, rows, cols))
-        approx = jnp.concatenate(sides, 1)
-        owned[:, span] = jnp.stack(sides, 0)
-        feedback_buffer[span] = gradients[span].astype(F32) + feedback[span] - approx
-        kept = [base[side, span].astype(F32) for side in range(2)]
-        weight_buffer[span] = (jnp.concatenate(kept, 1) - LEARN_RATE * approx).astype(BF16)
-        for which, (source, target) in enumerate(((feedback_buffer, new_feedback), (weight_buffer, weight))):
-            copy = pltpu.make_async_copy(source.at[span], target.at[span], sems.at[chunk, which])
-            copy.start()
-            copies.append(copy)
+    for side in range(2):
+        terms = ortho_terms[:, side * half : (side + 1) * half]
+        owned[side] = product(terms, right_terms[...], ((0,), (0,))).reshape(chips, rows, cols)
+    approx = jnp.concatenate([owned[side] for side in range(2)], 1)
+    feedback_buffer[...] = gradients[...].astype(F32) + feedback[...] - approx
+    copies = [pltpu.make_async_copy(feedback_buffer, new_feedback, sems.at[0])]
+    copies[0].start()
+    kept = jnp.concatenate([base[side].astype(F32) for side in range(2)], 1)
+    weight_buffer[...] = (kept - LEARN_RATE * approx).astype(BF16)
+    copies.append(pltpu.make_async_copy(weight_buffer, weight, sems.at[1]))
+    copies[1].start()
     moved = MOMENTUM_RATE * momentum[...] + owned[core, chip]
     new_momentum[...] = moved
     new_master[...] = master[...] - LEARN_RATE * moved
@@ -256,20 +238,19 @@
     sent, kept = pl.pallas_call(
         pack_kernel,
         out_shape=(
-            jax.ShapeDtypeStruct((chips + 1, owned, cols), BF16),
+            jax.ShapeDtypeStruct((chips, owned, cols), BF16),
             jax.ShapeDtypeStruct((chips, owned, cols), F32),
         ),
-        in_specs=[ANY] * 3,
+        in_specs=[ANY] * 2,
         out_specs=(VMEM, VMEM),
         scratch_shapes=[
             pltpu.VMEM(by_owner, BF16),
             pltpu.VMEM(by_owner, F32),
-            pltpu.VMEM(lines.shape, F32),
-            pltpu.SemaphoreType.DMA((CHUNKS + 1, 2)),
+            pltpu.SemaphoreType.DMA((CHUNKS, 2)),
         ],
         compiler_params=PACK,
         name="pack",
-    )(*halves, lines)
+    )(*halves)
     received = lax.ppermute(sent, "c", SWAP)
     paired = pl.pallas_call(
         pair_kernel,
@@ -285,11 +266,11 @@
     shared = pl.pallas_call(
         share_kernel,
         out_shape=jax.ShapeDtypeStruct((chips, owned, shared_cols), BF16),
-        in_specs=[VMEM] * 5,
+        in_specs=[VMEM] * 4,
         out_specs=VMEM,
         compiler_params=SMALL,
         name="share",
-    )(arrived, received, lines, momentum, master_owned)
+    )(arrived, lines, momentum, master_owned)
     near = exchange(shared, CHIPS)
     far = lax.ppermute(near, "c", SWAP)
     left = pl.pallas_call(
@@ -337,7 +318,7 @@
             pltpu.VMEM(by_pair, BF16),
             pltpu.VMEM((2, chips, owned, cols), BF16),
             pltpu.VMEM((2, chips, owned, cols), F32),
-            pltpu.SemaphoreType.DMA((CHUNKS, 2)),
+            pltpu.SemaphoreType.DMA((2,)),
         ],
         compiler_params=LARGE,
         name="finish",

time: 94.3 us -> 93.8 us (level)
  no operation moved by 1% of the time
where the time goes in v6:
time: 93.8 us; the launch traced here: 92.7 us
  blocking collectives  59.5 us (63%)
  starting transfers between devices  18.1 us (19%)
  Pallas kernels  8.03 us (9%)
  waiting for transfers between devices  4.84 us (5%)
    all_to_all x3, blocking collectives, exchange(): return lax.all_to_all(array, axis, 0, 0, tiled=True)  59.5 us
    ppermute x1, starting transfers between devices, shards(): received = lax.ppermute(sent, 'c', SWAP)  8.75 us
    ppermute x1, starting transfers between devices, shards(): far = lax.ppermute(near, 'c', SWAP)  5.85 us
    pallas_call x1, Pallas kernels, shards(): pl.pallas_call(functools.partial(finish_kernel, replicas=replicas), out_s...  3.94 us
    all_to_all x1, waiting for transfers between devices, exchange(): return lax.all_to_all(array, axis, 0, 0, tiled=True)  3.7 us
    all_to_all x1, starting transfers between devices, exchange(): return lax.all_to_all(array, axis, 0, 0, tiled=True)  3.54 us
  transfers between devices with their start and end apart: 3, of which 2 were waited for; matrix products, arithmetic and copies ran while one was open for 1% of the time, Pallas kernels for 1%

profile of v6, /device:TPU:1, one launch (start us, length us, event | category | flops | bytes accessed | tf_op | source)
XLA Modules:
  0.0 92.7 jit_solution(7142293456193321007)
XLA Ops:
  0.6 1.5 %pack.1 = (bf16[64,8,256]{2,1,0:T(8,128)(2,1)S(1)}, f32[64,8,256]{2,1,0:T(8,128)S(1)}) custom-call(bf16[64,2,8,256]{3,2,1,0:T(8,128)(2,1)} %bitcast.13, f32[64,2,8,256]{3,2,1,0:T(8,128)} %bitcast.11), custom_call_target="tpu_custom_call" | custom-call | tf_op jit(solution)/shard_map/pack/pallas_call | solution.py:238
  2.1 8.8 %collective-permute-start = (bf16[64,8,256]{2,1,0:T(8,128)(2,1)S(1)}, bf16[64,8,256]{2,1,0:T(8,128)(2,1)S(1)}, u32[]{:S(2)}, u32[]{:S(2)}) collective-permute-start(bf16[64,8,256]{2,1,0:T(8,128)(2,1)S(1)} %get-tuple-element.15), channel_id=1, source_target_pairs={{0,4},{4,0},{1,5},{5,1},{2,6},{6,2},{3,7},{7,3},{8,12},{12,8},{9,1... | collective-permute-start | bytes 786440 | tf_op jit(solution)/shard_map/ppermute | solution.py:254
  10.9 1.1 %collective-permute-done.received = bf16[64,8,256]{2,1,0:T(8,128)(2,1)S(1)} collective-permute-done((bf16[64,8,256]{2,1,0:T(8,128)(2,1)S(1)}, bf16[64,8,256]{2,1,0:T(8,128)(2,1)S(1)}, u32[]{:S(2)}, u32[]{:S(2)}) %collective-permute-start) | collective-permute-done | bytes 262176 | tf_op jit(solution)/shard_map/ppermute | solution.py:254
  12.0 0.0 copy-start.2
  12.1 0.0 copy-start.3
  12.1 0.0 copy-start.5
  12.1 24.0 %all_to_all.20.arrived = bf16[64,8,256]{2,1,0:T(8,128)(2,1)S(1)} all-to-all(bf16[64,8,256]{2,1,0:T(8,128)(2,1)S(1)} %pair.1), channel_id=1, replica_groups=mesh['y'=8,'z'=8,'c'=2,'tp'=4] {'y','z'}, dimensions={0} | all-to-all | bytes 524288 | tf_op jit(solution)/shard_map/all_to_all | solution.py:36
  36.1 0.0 copy-done.2
  36.1 0.0 copy-done.3
  36.1 0.0 copy-done.5
  36.1 0.1 share.1
  36.2 0.0 copy-start.4
  36.2 23.8 %all_to_all.21.near = bf16[64,8,640]{2,1,0:T(8,128)(2,1)S(1)} all-to-all(bf16[64,8,640]{2,1,0:T(8,128)(2,1)S(1)} %share.1), channel_id=1, replica_groups=mesh['y'=8,'z'=8,'c'=2,'tp'=4] {'y','z'}, dimensions={0} | all-to-all | bytes 1310720 | tf_op jit(solution)/shard_map/all_to_all | solution.py:36
  60.0 5.9 %collective-permute-start.1 = (bf16[64,8,640]{2,1,0:T(8,128)(2,1)S(1)}, bf16[64,8,640]{2,1,0:T(8,128)(2,1)S(1)}, u32[]{:S(2)}, u32[]{:S(2)}) collective-permute-start(bf16[64,8,640]{2,1,0:T(8,128)(2,1)S(1)} %all_to_all.21.near), channel_id=1, source_target_pairs={{0,4},{4,0},{1,5},{5,1},{2,6},{6,2},{3,7},{7,3},{8,12},{12,8},{9,1... | collective-permute-start | bytes 1966088 | tf_op jit(solution)/shard_map/ppermute | solution.py:275
  65.9 0.0 copy-done.4
  65.9 0.2 left.1
  66.1 11.8 %all_to_all.22.arrived = bf16[8,40,512]{2,1,0:T(8,128)(2,1)S(1)} all-to-all(bf16[8,40,512]{2,1,0:T(8,128)(2,1)S(1)} %left.1), channel_id=1, replica_groups=mesh['y'=8,'z'=8,'c'=2,'tp'=4] {'c','tp'}, dimensions={0} | all-to-all | bytes 655360 | tf_op jit(solution)/shard_map/all_to_all | solution.py:36
  77.9 0.0 collective-permute-done.1.far
  77.9 0.0 copy-start.1
  77.9 1.3 %power.1.after = bf16[4,32,1024]{2,1,0:T(8,128)(2,1)} custom-call(bf16[8,40,512]{2,1,0:T(8,128)(2,1)S(1)} %all_to_all.22.arrived, bf16[64,8,640]{2,1,0:T(8,128)(2,1)S(1)} %all_to_all.21.near, bf16[64,8,640]{2,1,0:T(8,128)(2,1)S(1)} %collective-permute-done.1.far), custom_call_target="tpu_custom_call" | custom-call | tf_op jit(solution)/shard_map/power/pallas_call | solution.py:285
  79.1 0.0 copy-start
  79.1 3.5 %all-to-all-start.3 = ((bf16[4,32,1024]{2,1,0:T(8,128)(2,1)}), bf16[4,32,1024]{2,1,0:T(8,128)(2,1)S(1)}, u32[]{:S(2)}, u32[]{:S(2)}) async-start(bf16[4,32,1024]{2,1,0:T(8,128)(2,1)} %power.1.after), calls=%async_computation.3 | async-start | bytes 524288 | tf_op jit(solution)/shard_map/all_to_all | solution.py:36
  82.7 0.0 copy-start.7
  82.7 1.0 %factor.1 = (f32[32,32]{1,0:T(8,128)S(1)}, f32[20,1,128]{2,1,0:T(1,128)S(1)}) custom-call(bf16[8,40,512]{2,1,0:T(8,128)(2,1)S(1)} %all_to_all.22.arrived, bf16[4,32,1024]{2,1,0:T(8,128)(2,1)} %power.1.after), custom_call_target="tpu_custom_call" | custom-call | tf_op jit(solution)/shard_map/factor/pallas_call | solution.py:293
  83.7 0.0 copy-start.6
  83.7 0.0 copy-done.7
  83.7 0.7 copy-done.6
  84.4 0.6 multiply_subtract_fusion
  85.0 3.7 %all-to-all-done.3.parts = bf16[4,32,1024]{2,1,0:T(8,128)(2,1)S(1)} async-done(((bf16[4,32,1024]{2,1,0:T(8,128)(2,1)}), bf16[4,32,1024]{2,1,0:T(8,128)(2,1)S(1)}, u32[]{:S(2)}, u32[]{:S(2)}) %all-to-all-start.3) | async-done | bytes 262176 | tf_op jit(solution)/shard_map/all_to_all | solution.py:36
  88.7 0.0 copy-done.1
  88.7 0.0 copy-done
  88.7 3.9 %finish.1 = (f32[64,16,256]{2,1,0:T(8,128)}, bf16[64,16,256]{2,1,0:T(8,128)(2,1)}, f32[8,256]{1,0:T(8,128)}, f32[8,256]{1,0:T(8,128)}) custom-call(bf16[4,32,1024]{2,1,0:T(8,128)(2,1)S(1)} %all-to-all-done.3.parts, f32[32,32]{1,0:T(8,128)S(1)} %get-tuple-element.16.inverse_one, bf16[64,8,640]{2,1,0:T(8,128)(2,1)S(1)} %all_to_all.21.near, ...), custom_call_target="tpu_custom_call" | custom-call | tf_op jit(solution)/shard_map/finish/pallas_call | solution.py:304
  (2 shorter events, 0.1 us)
Async XLA Ops:
  2.1 9.9 %collective-permute-start = (bf16[64,8,256]{2,1,0:T(8,128)(2,1)S(1)}, bf16[64,8,256]{2,1,0:T(8,128)(2,1)S(1)}, u32[]{:S(2)}, u32[]{:S(2)}) collective-permute-start(bf16[64,8,256]{2,1,0:T(8,128)(2,1)S(1)} %get-tuple-element.15), channel_id=1, source_target_pairs={{0,4},{4,0},{1,5},{5,1},{2,6},{6,2},{3,7},{7,3},{8,12},{12,8},{9,1... | collective-permute-start | bytes 786440 | tf_op jit(solution)/shard_map/ppermute | solution.py:254
  12.0 24.0 %copy-start.2 = (f32[8,256]{1,0:T(8,128)S(1)}, f32[8,256]{1,0:T(8,128)}, u32[]{:S(2)}) copy-start(f32[8,256]{1,0:T(8,128)} %momentum.3) | copy-start | bytes 24580
  12.1 24.0 %copy-start.3 = (f32[8,256]{1,0:T(8,128)S(1)}, f32[8,256]{1,0:T(8,128)}, u32[]{:S(2)}) copy-start(f32[8,256]{1,0:T(8,128)} %master.3) | copy-start | bytes 24580
  12.1 24.0 %copy-start.5 = (f32[1,2560]{1,0:T(1,128)S(1)}, f32[1,2560]{1,0:T(1,128)}, u32[]{:S(2)}) copy-start(f32[1,2560]{1,0:T(1,128)} %param.13) | copy-start | bytes 30724
  36.2 29.7 %copy-start.4 = (f32[256,32]{0,1:T(8,128)S(1)}, f32[256,32]{0,1:T(8,128)}, u32[]{:S(2)}) copy-start(f32[256,32]{0,1:T(8,128)} %param.10) | copy-start | bytes 98308
  60.0 17.9 %collective-permute-start.1 = (bf16[64,8,640]{2,1,0:T(8,128)(2,1)S(1)}, bf16[64,8,640]{2,1,0:T(8,128)(2,1)S(1)}, u32[]{:S(2)}, u32[]{:S(2)}) collective-permute-start(bf16[64,8,640]{2,1,0:T(8,128)(2,1)S(1)} %all_to_all.21.near), channel_id=1, source_target_pairs={{0,4},{4,0},{1,5},{5,1},{2,6},{6,2},{3,7},{7,3},{8,12},{12,8},{9,1... | collective-permute-start | bytes 1966088 | tf_op jit(solution)/shard_map/ppermute | solution.py:275
  77.9 10.9 %copy-start.1 = (bf16[1,1024,256]{2,1,0:T(8,128)(2,1)S(1)}, bf16[1,1024,256]{2,1,0:T(8,128)(2,1)}, u32[]{:S(2)}) copy-start(bf16[1,1024,256]{2,1,0:T(8,128)(2,1)} %param.8) | copy-start | bytes 1572868
  79.1 9.6 %copy-start = (f32[1,1024,256]{2,1,0:T(8,128)S(1)}, f32[1,1024,256]{2,1,0:T(8,128)}, u32[]{:S(2)}) copy-start(f32[1,1024,256]{2,1,0:T(8,128)} %param.9) | copy-start | bytes 3145732
  79.1 9.6 %all-to-all-start.3 = ((bf16[4,32,1024]{2,1,0:T(8,128)(2,1)}), bf16[4,32,1024]{2,1,0:T(8,128)(2,1)S(1)}, u32[]{:S(2)}, u32[]{:S(2)}) async-start(bf16[4,32,1024]{2,1,0:T(8,128)(2,1)} %power.1.after), calls=%async_computation.3 | async-start | bytes 524288 | tf_op jit(solution)/shard_map/all_to_all | solution.py:36
  82.7 1.1 %copy-start.7 = (f32[2560]{0:T(1024)S(1)}, f32[2560]{0:T(1024)}, u32[]{:S(2)}) copy-start(f32[2560]{0:T(1024)} %param.15) | copy-start | bytes 30724
  83.7 0.7 copy-start.6

commit v7 on v6

--- a/solution.py
+++ b/solution.py
@@ -163,6 +163,7 @@
     inverse_one,
     near,
     far,
+    far_base,
     gradients,
     feedback,
     momentum,
@@ -185,8 +186,8 @@
     chips, pair, cols = feedback.shape
     rows = pair // 2
     half = chips * rows
-    for side, ref in ((core, near), (1 - core, far)):
-        base[side] = ref[:, :, cols + LANES :]
+    base[core] = near[:, :, cols + LANES :]
+    base[1 - core] = far_base[...]
     left = product(inverse_one[...], jnp.sum(parts[...].astype(F32), axis=0), ((1,), (0,)), PRECISE)
     ortho = product(gram_inverse(left), left, ((1,), (0,)), PRECISE)
     right = times_exact(ortho[:, :half], matrix_of(near, cols), ((1,), (0,)))
@@ -272,7 +273,7 @@
         name="share",
     )(arrived, lines, momentum, master_owned)
     near = exchange(shared, CHIPS)
-    far = lax.ppermute(near, "c", SWAP)
+    far = lax.ppermute(near[:, :, :cols], "c", SWAP)
     left = pl.pallas_call(
         left_kernel,
         out_shape=jax.ShapeDtypeStruct((2 * tp, rank + 8, half), BF16),
@@ -299,6 +300,7 @@
         name="factor",
     )(left, parts)
     parts = exchange(parts, "tp")
+    far_base = lax.ppermute(near[:, :, cols + LANES :], "c", SWAP)
     vector_sum = vector.reshape(-1)
 
     new_feedback, weight, new_momentum, new_master = pl.pallas_call(
@@ -309,7 +311,7 @@
             jax.ShapeDtypeStruct(momentum.shape, F32),
             jax.ShapeDtypeStruct(momentum.shape, F32),
         ),
-        in_specs=[VMEM] * 8,
+        in_specs=[VMEM] * 9,
         out_specs=(ANY, ANY, VMEM, VMEM),
         scratch_shapes=[
             pltpu.VMEM((3 * rank, rows), BF16),
@@ -327,6 +329,7 @@
         inverse_one,
         near,
         far,
+        far_base,
         gradients.reshape(by_pair),
         feedback.reshape(by_pair),
         momentum,

time: 93.8 us -> 92.5 us (0.986)
  blocking collectives: 59.5 us -> 47.8 us
  starting transfers between devices: 18.1 us -> 25 us
  waiting for transfers between devices: 4.84 us -> 6.95 us
    all_to_all x3 -> x2, blocking collectives: 59.5 us -> 47.8 us  [exchange(): return lax.all_to_all(array, axis, 0, 0, tiled=True)]
    all_to_all x1 -> x2, starting transfers between devices: 3.54 us -> 11.8 us  [exchange(): return lax.all_to_all(array, axis, 0, 0, tiled=True)]
    all_to_all x1 -> x2, waiting for transfers between devices: 3.7 us -> 5.8 us  [exchange(): return lax.all_to_all(array, axis, 0, 0, tiled=True)]
    ppermute x1 -> x2, starting transfers between devices: 5.85 us -> 4.45 us  [the longest x1 2.54 us: shards(): far_base = lax.ppermute(near[:, :, cols + LANES:], 'c', SWAP)]
  transfers between devices with their start and end apart: 3 -> 5, of which waited for: 2 -> 3; matrix products, arithmetic and copies ran while one was open for 1% -> 2% of each run, Pallas kernels for 1% -> 2%
where the time goes in v7:
time: 92.5 us; the launch traced here: 91.3 us
  blocking collectives  47.8 us (52%)
  starting transfers between devices  25 us (27%)
  Pallas kernels  8.76 us (9%)
  waiting for transfers between devices  6.95 us (8%)
  local copies, waits for them, and re-layouts  1.44 us (2%)
    all_to_all x2, blocking collectives, exchange(): return lax.all_to_all(array, axis, 0, 0, tiled=True)  47.8 us
    all_to_all x2, starting transfers between devices, exchange(): return lax.all_to_all(array, axis, 0, 0, tiled=True)  11.8 us
    ppermute x1, starting transfers between devices, shards(): received = lax.ppermute(sent, 'c', SWAP)  8.75 us
    all_to_all x2, waiting for transfers between devices, exchange(): return lax.all_to_all(array, axis, 0, 0, tiled=True)  5.8 us
    pallas_call x1, Pallas kernels, shards(): pl.pallas_call(functools.partial(finish_kernel, replicas=replicas), out_s...  3.94 us
    ppermute x1, starting transfers between devices, shards(): far_base = lax.ppermute(near[:, :, cols + LANES:], 'c', SWAP)  2.54 us
    ppermute x1, starting transfers between devices, shards(): far = lax.ppermute(near[:, :, :cols], 'c', SWAP)  1.91 us
  transfers between devices with their start and end apart: 5, of which 3 were waited for; matrix products, arithmetic and copies ran while one was open for 2% of the time, Pallas kernels for 2%

profile of v7, /device:TPU:1, one launch (start us, length us, event | category | flops | bytes accessed | tf_op | source)
XLA Modules:
  0.0 91.3 jit_solution(14791558578103665269)
XLA Ops:
  0.6 1.5 %pack.1 = (bf16[64,8,256]{2,1,0:T(8,128)(2,1)S(1)}, f32[64,8,256]{2,1,0:T(8,128)S(1)}) custom-call(bf16[64,2,8,256]{3,2,1,0:T(8,128)(2,1)} %bitcast.13, f32[64,2,8,256]{3,2,1,0:T(8,128)} %bitcast.11), custom_call_target="tpu_custom_call" | custom-call | tf_op jit(solution)/shard_map/pack/pallas_call | solution.py:239
  2.1 8.8 %collective-permute-start = (bf16[64,8,256]{2,1,0:T(8,128)(2,1)S(1)}, bf16[64,8,256]{2,1,0:T(8,128)(2,1)S(1)}, u32[]{:S(2)}, u32[]{:S(2)}) collective-permute-start(bf16[64,8,256]{2,1,0:T(8,128)(2,1)S(1)} %get-tuple-element.15), channel_id=1, source_target_pairs={{0,4},{4,0},{1,5},{5,1},{2,6},{6,2},{3,7},{7,3},{8,12},{12,8},{9,1... | collective-permute-start | bytes 786440 | tf_op jit(solution)/shard_map/ppermute | solution.py:255
  10.9 1.1 %collective-permute-done.received = bf16[64,8,256]{2,1,0:T(8,128)(2,1)S(1)} collective-permute-done((bf16[64,8,256]{2,1,0:T(8,128)(2,1)S(1)}, bf16[64,8,256]{2,1,0:T(8,128)(2,1)S(1)}, u32[]{:S(2)}, u32[]{:S(2)}) %collective-permute-start) | collective-permute-done | bytes 262176 | tf_op jit(solution)/shard_map/ppermute | solution.py:255
  12.0 0.0 copy-start.2
  12.1 0.0 copy-start.3
  12.1 0.0 copy-start.5
  12.1 24.0 %all_to_all.20.arrived = bf16[64,8,256]{2,1,0:T(8,128)(2,1)S(1)} all-to-all(bf16[64,8,256]{2,1,0:T(8,128)(2,1)S(1)} %pair.1), channel_id=1, replica_groups=mesh['y'=8,'z'=8,'c'=2,'tp'=4] {'y','z'}, dimensions={0} | all-to-all | bytes 524288 | tf_op jit(solution)/shard_map/all_to_all | solution.py:36
  36.1 0.0 copy-done.2
  36.1 0.0 copy-done.3
  36.1 0.0 copy-done.5
  36.1 0.1 share.1
  36.2 0.0 copy-start.4
  36.2 23.8 %all_to_all.21.near = bf16[64,8,640]{2,1,0:T(8,128)(2,1)S(1)} all-to-all(bf16[64,8,640]{2,1,0:T(8,128)(2,1)S(1)} %share.1), channel_id=1, replica_groups=mesh['y'=8,'z'=8,'c'=2,'tp'=4] {'y','z'}, dimensions={0} | all-to-all | bytes 1310720 | tf_op jit(solution)/shard_map/all_to_all | solution.py:36
  60.0 0.0 copy-done.4
  60.0 0.9 %left.1 = bf16[8,40,512]{2,1,0:T(8,128)(2,1)} custom-call(bf16[64,8,640]{2,1,0:T(8,128)(2,1)S(1)} %all_to_all.21.near, f32[32,256]{1,0:T(8,128)S(1)} %bitcast.15), custom_call_target="tpu_custom_call" | custom-call | tf_op jit(solution)/shard_map/left/pallas_call | solution.py:277
  60.9 8.3 %all-to-all-start.2 = ((bf16[8,40,512]{2,1,0:T(8,128)(2,1)}), bf16[8,40,512]{2,1,0:T(8,128)(2,1)S(1)}, u32[]{:S(2)}, u32[]{:S(2)}) async-start(bf16[8,40,512]{2,1,0:T(8,128)(2,1)} %left.1), calls=%async_computation.2 | async-start | bytes 655360 | tf_op jit(solution)/shard_map/all_to_all | solution.py:36
  69.2 0.7 fusion
  69.9 1.9 %collective-permute-start.1 = (bf16[64,8,256]{2,1,0:T(8,128)(2,1)S(1)}, bf16[64,8,256]{2,1,0:T(8,128)(2,1)S(1)}, u32[]{:S(2)}, u32[]{:S(2)}) collective-permute-start(bf16[64,8,256]{2,1,0:T(8,128)(2,1)S(1)} %get-tuple-element.25), channel_id=1, source_target_pairs={{0,4},{4,0},{1,5},{5,1},{2,6},{6,2},{3,7},{7,3},{8,12},{12,8},{9,1... | collective-permute-start | bytes 786440 | tf_op jit(solution)/shard_map/ppermute | solution.py:276
  71.9 0.0 copy-start
  71.9 2.5 %collective-permute-start.2 = (bf16[64,8,256]{2,1,0:T(8,128)(2,1)}, bf16[64,8,256]{2,1,0:T(8,128)(2,1)S(1)}, u32[]{:S(2)}, u32[]{:S(2)}) collective-permute-start(bf16[64,8,256]{2,1,0:T(8,128)(2,1)} %get-tuple-element.24), channel_id=1, source_target_pairs={{0,4},{4,0},{1,5},{5,1},{2,6},{6,2},{3,7},{7,3},{8,12},{12,8},{9,1... | collective-permute-start | bytes 786440 | tf_op jit(solution)/shard_map/ppermute | solution.py:303
  74.4 0.0 collective-permute-done.1.far
  74.4 2.0 %all-to-all-done.2.arrived = bf16[8,40,512]{2,1,0:T(8,128)(2,1)S(1)} async-done(((bf16[8,40,512]{2,1,0:T(8,128)(2,1)}), bf16[8,40,512]{2,1,0:T(8,128)(2,1)S(1)}, u32[]{:S(2)}, u32[]{:S(2)}) %all-to-all-start.2) | async-done | bytes 327712 | tf_op jit(solution)/shard_map/all_to_all | solution.py:36
  76.4 1.3 %power.1.after = bf16[4,32,1024]{2,1,0:T(8,128)(2,1)} custom-call(bf16[8,40,512]{2,1,0:T(8,128)(2,1)S(1)} %all-to-all-done.2.arrived, bf16[64,8,640]{2,1,0:T(8,128)(2,1)S(1)} %all_to_all.21.near, bf16[64,8,256]{2,1,0:T(8,128)(2,1)S(1)} %collective-permute-done.1.far), custom_call_target="tpu_custom_call" | custom-call | tf_op jit(solution)/shard_map/power/pallas_call | solution.py:286
  77.7 3.5 %all-to-all-start.3 = ((bf16[4,32,1024]{2,1,0:T(8,128)(2,1)}), bf16[4,32,1024]{2,1,0:T(8,128)(2,1)S(1)}, u32[]{:S(2)}, u32[]{:S(2)}) async-start(bf16[4,32,1024]{2,1,0:T(8,128)(2,1)} %power.1.after), calls=%async_computation.3 | async-start | bytes 524288 | tf_op jit(solution)/shard_map/all_to_all | solution.py:36
  81.2 0.0 copy-start.7
  81.2 1.0 %factor.1 = (f32[32,32]{1,0:T(8,128)S(1)}, f32[20,1,128]{2,1,0:T(1,128)S(1)}) custom-call(bf16[8,40,512]{2,1,0:T(8,128)(2,1)S(1)} %all-to-all-done.2.arrived, bf16[4,32,1024]{2,1,0:T(8,128)(2,1)} %power.1.after), custom_call_target="tpu_custom_call" | custom-call | tf_op jit(solution)/shard_map/factor/pallas_call | solution.py:294
  82.3 0.0 copy-done.7
  82.3 0.7 copy-done.6
  83.0 0.6 multiply_subtract_fusion
  83.6 0.0 collective-permute-done.2.far_base
  83.6 3.8 %all-to-all-done.3.parts = bf16[4,32,1024]{2,1,0:T(8,128)(2,1)S(1)} async-done(((bf16[4,32,1024]{2,1,0:T(8,128)(2,1)}), bf16[4,32,1024]{2,1,0:T(8,128)(2,1)S(1)}, u32[]{:S(2)}, u32[]{:S(2)}) %all-to-all-start.3) | async-done | bytes 262176 | tf_op jit(solution)/shard_map/all_to_all | solution.py:36
  87.4 3.9 %finish.1 = (f32[64,16,256]{2,1,0:T(8,128)}, bf16[64,16,256]{2,1,0:T(8,128)(2,1)}, f32[8,256]{1,0:T(8,128)}, f32[8,256]{1,0:T(8,128)}) custom-call(bf16[4,32,1024]{2,1,0:T(8,128)(2,1)S(1)} %all-to-all-done.3.parts, f32[32,32]{1,0:T(8,128)S(1)} %get-tuple-element.16.inverse_one, bf16[64,8,640]{2,1,0:T(8,128)(2,1)S(1)} %all_to_all.21.near, ...), custom_call_target="tpu_custom_call" | custom-call | tf_op jit(solution)/shard_map/finish/pallas_call | solution.py:306
  (6 shorter events, 0.1 us)
Async XLA Ops:
  2.1 9.9 %collective-permute-start = (bf16[64,8,256]{2,1,0:T(8,128)(2,1)S(1)}, bf16[64,8,256]{2,1,0:T(8,128)(2,1)S(1)}, u32[]{:S(2)}, u32[]{:S(2)}) collective-permute-start(bf16[64,8,256]{2,1,0:T(8,128)(2,1)S(1)} %get-tuple-element.15), channel_id=1, source_target_pairs={{0,4},{4,0},{1,5},{5,1},{2,6},{6,2},{3,7},{7,3},{8,12},{12,8},{9,1... | collective-permute-start | bytes 786440 | tf_op jit(solution)/shard_map/ppermute | solution.py:255
  12.0 24.0 %copy-start.2 = (f32[8,256]{1,0:T(8,128)S(1)}, f32[8,256]{1,0:T(8,128)}, u32[]{:S(2)}) copy-start(f32[8,256]{1,0:T(8,128)} %momentum.3) | copy-start | bytes 24580
  12.1 24.0 %copy-start.3 = (f32[8,256]{1,0:T(8,128)S(1)}, f32[8,256]{1,0:T(8,128)}, u32[]{:S(2)}) copy-start(f32[8,256]{1,0:T(8,128)} %master.3) | copy-start | bytes 24580
  12.1 24.0 %copy-start.5 = (f32[1,2560]{1,0:T(1,128)S(1)}, f32[1,2560]{1,0:T(1,128)}, u32[]{:S(2)}) copy-start(f32[1,2560]{1,0:T(1,128)} %param.13) | copy-start | bytes 30724
  36.2 23.8 %copy-start.4 = (f32[256,32]{0,1:T(8,128)S(1)}, f32[256,32]{0,1:T(8,128)}, u32[]{:S(2)}) copy-start(f32[256,32]{0,1:T(8,128)} %param.10) | copy-start | bytes 98308
  60.9 15.5 %all-to-all-start.2 = ((bf16[8,40,512]{2,1,0:T(8,128)(2,1)}), bf16[8,40,512]{2,1,0:T(8,128)(2,1)S(1)}, u32[]{:S(2)}, u32[]{:S(2)}) async-start(bf16[8,40,512]{2,1,0:T(8,128)(2,1)} %left.1), calls=%async_computation.2 | async-start | bytes 655360 | tf_op jit(solution)/shard_map/all_to_all | solution.py:36
  69.9 4.5 %collective-permute-start.1 = (bf16[64,8,256]{2,1,0:T(8,128)(2,1)S(1)}, bf16[64,8,256]{2,1,0:T(8,128)(2,1)S(1)}, u32[]{:S(2)}, u32[]{:S(2)}) collective-permute-start(bf16[64,8,256]{2,1,0:T(8,128)(2,1)S(1)} %get-tuple-element.25), channel_id=1, source_target_pairs={{0,4},{4,0},{1,5},{5,1},{2,6},{6,2},{3,7},{7,3},{8,12},{12,8},{9,1... | collective-permute-start | bytes 786440 | tf_op jit(solution)/shard_map/ppermute | solution.py:276
  71.9 15.5 %copy-start = (f32[1,1024,256]{2,1,0:T(8,128)S(1)}, f32[1,1024,256]{2,1,0:T(8,128)}, u32[]{:S(2)}) copy-start(f32[1,1024,256]{2,1,0:T(8,128)} %param.9) | copy-start | bytes 3145732
  71.9 11.7 %collective-permute-start.2 = (bf16[64,8,256]{2,1,0:T(8,128)(2,1)}, bf16[64,8,256]{2,1,0:T(8,128)(2,1)S(1)}, u32[]{:S(2)}, u32[]{:S(2)}) collective-permute-start(bf16[64,8,256]{2,1,0:T(8,128)(2,1)} %get-tuple-element.24), channel_id=1, source_target_pairs={{0,4},{4,0},{1,5},{5,1},{2,6},{6,2},{3,7},{7,3},{8,12},{12,8},{9,1... | collective-permute-start | bytes 786440 | tf_op jit(solution)/shard_map/ppermute | solution.py:303
  77.7 9.7 %copy-start.1 = (bf16[1,1024,256]{2,1,0:T(8,128)(2,1)S(1)}, bf16[1,1024,256]{2,1,0:T(8,128)(2,1)}, u32[]{:S(2)}) copy-start(bf16[1,1024,256]{2,1,0:T(8,128)(2,1)} %param.8) | copy-start | bytes 1572868
  77.7 9.7 %all-to-all-start.3 = ((bf16[4,32,1024]{2,1,0:T(8,128)(2,1)}), bf16[4,32,1024]{2,1,0:T(8,128)(2,1)S(1)}, u32[]{:S(2)}, u32[]{:S(2)}) async-start(bf16[4,32,1024]{2,1,0:T(8,128)(2,1)} %power.1.after), calls=%async_computation.3 | async-start | bytes 524288 | tf_op jit(solution)/shard_map/all_to_all | solution.py:36
  81.2 1.1 %copy-start.7 = (f32[2560]{0:T(1024)S(1)}, f32[2560]{0:T(1024)}, u32[]{:S(2)}) copy-start(f32[2560]{0:T(1024)} %param.15) | copy-start | bytes 30724
  82.3 0.7 copy-start.6
